TPU v7x, 256 devices: a whole 4x4x8 slice. The times are simulated.
256 devices in a mesh: wide: 32 (over y, x, core), narrow: 8 (over z).
Axes of the slice: x: 4, y: 4, z: 8, core: 2. Of those that a mesh axis runs over, the one named last changes fastest.
Arguments:
- expression: bfloat16 [4000, 393216], P(None, ('wide', 'narrow')), may hold values from -60 to 60
- sketch_map: bfloat16 [64, 4000], replicated, may hold values from -0.09375 to 0.09375
Outputs:
- projected: float32 [64, 4000], P(None, 'narrow')
All inputs are finite; a program needn't handle non-finite values.
Results may differ from a plain program's by a relative error of at most 0.00037.
Values sent between devices are 32-bit elements; how exact they have to be, the bound alone decides.
No kernel may reach another device: no remote copies, remote signals or barrier semaphores. Data moves between devices by JAX's collectives and lax.ppermute only.
A program may use at most 64 MiB of HBM per device.

v0:
```python
import jax
import jax.numpy as jnp
from jax import lax
from jax.sharding import PartitionSpec as P


def split_up(array, dim, count):
    before, after = (array.shape[:dim], array.shape[dim + 1 :])
    return jnp.moveaxis(array.reshape(*before, count, -1, *after), dim, 0)


def summed_on_arrival(array, axis, dim):
    parts = split_up(array, dim, lax.axis_size(axis))
    arrived = lax.all_to_all(parts, axis, split_axis=0, concat_axis=0, tiled=True)
    return arrived.sum(axis=0)


def copy_for_each(array, axis):
    count = lax.axis_size(axis)
    return lax.all_to_all(
        jnp.broadcast_to(array[None], (count, *array.shape)), axis, 0, 0, tiled=True
    )


def taken_together(array, axis):
    return copy_for_each(array, axis).sum(axis=0)


def on_device(expression, sketch_map):
    sketched = jnp.dot(sketch_map, expression, preferred_element_type=jnp.float32).astype(
        jnp.bfloat16
    )
    products = lax.dot_general(
        sketched, expression, (((1,), (1,)), ((), ())), preferred_element_type=jnp.float32
    )
    gram_local = lax.dot_general(
        sketched, sketched, (((1,), (1,)), ((), ())), preferred_element_type=jnp.float32
    )
    rows_count = products.shape[0]
    gene_count = products.shape[1]
    group_count = lax.axis_size("narrow")
    share_width = gene_count // group_count
    blocks = products.reshape(rows_count, group_count, share_width)
    repeated = jnp.broadcast_to(gram_local[:, None, :], (rows_count, group_count, rows_count))
    packed = jnp.concatenate([blocks, repeated], axis=2).reshape(
        rows_count, group_count * (share_width + rows_count)
    )
    group_sum = summed_on_arrival(packed, "narrow", 1)
    joined = taken_together(group_sum, "wide")
    own_genes = joined[:, :share_width]
    gram = joined[:, share_width:]
    lower = jnp.linalg.cholesky(gram)
    projected = lax.linalg.triangular_solve(lower, own_genes, left_side=True, lower=True)
    return projected


def solution(mesh):
    placed = (P(None, ("wide", "narrow")), P())
    return jax.shard_map(
        on_device, mesh=mesh, in_specs=placed, out_specs=P(None, "narrow"), check_vma=False
    )
```

profile of v0, /device:TPU:1, one launch (start us, length us, event | category | flops | bytes accessed | tf_op | source)
XLA Modules:
  0.0 144.0 jit_solution(17231348267998548586)
XLA Ops:
  0.0 0.0 copy-start
  0.0 0.0 copy-start.1
  0.0 1.0 copy-done
  1.0 7.1 %convolution_convert_fusion = bf16[64,1536]{1,0:T(8,128)(2,1)S(1)} fusion(bf16[64,4000]{1,0:T(8,128)(2,1)S(1)} %copy-done, bf16[4000,1536]{1,0:T(8,128)(2,1)} %param.2), kind=kOutput, calls=%fused_computation | convolution fusion | flops 786530304 | bytes 12996608 | tf_op jit(solution)/shard_map/dot_general | solution.py:30
  8.2 0.2 fusion.6
  8.4 0.0 copy-done.1
  8.4 3.8 %fusion.5 = f32[64,4000]{1,0:T(8,128)S(1)} fusion(bf16[64,1536]{1,0:T(8,128)(2,1)S(1)} %convolution_convert_fusion, bf16[4000,1536]{1,0:T(8,128)(2,1)S(1)} %copy-done.1), kind=kOutput, calls=%fused_computation.13 | convolution fusion | flops 786432000 | bytes 13508608 | tf_op jit(solution)/shard_map/dot_general | solution.py:33
  12.2 1.0 reshape.14
  13.2 0.6 copy.6
  13.8 0.2 maximum_bitcast_fusion
  14.0 41.7 %all_to_all.10 = f32[8,64,564]{2,1,0:T(8,128)S(1)} all-to-all(f32[8,64,564]{2,1,0:T(8,128)S(1)} %maximum_bitcast_fusion), channel_id=1, replica_groups=mesh['wide'=32,'narrow'=8] {'narrow'}, dimensions={0} | all-to-all | bytes 2310144 | tf_op jit(solution)/shard_map/all_to_all | solution.py:14
  55.7 0.1 reduce_sum.18
  55.8 0.6 broadcast_in_dim.6
  56.4 71.6 %all_to_all.11 = f32[32,64,564]{2,1,0:T(8,128)} all-to-all(f32[32,64,564]{2,1,0:T(8,128)S(1)} %broadcast_in_dim.6), channel_id=1, replica_groups=mesh['wide'=32,'narrow'=8] {'wide'}, dimensions={0} | all-to-all | bytes 9240576 | tf_op jit(solution)/shard_map/all_to_all | solution.py:20
  127.9 2.8 %reduce_sum.19 = f32[64,564]{1,0:T(8,128)S(1)} reduce(f32[32,64,564]{2,1,0:T(8,128)} %all_to_all.11, f32[]{:T(128)} %constant.38.clone.1), dimensions={0}, to_apply=%region_1.0 | reduce | flops 1118976 | bytes 4764676 | tf_op jit(solution)/shard_map/reduce_sum | solution.py:26
  130.7 0.1 slice.16
  130.8 0.1 copy.9
  130.8 0.1 fusion.4
  130.9 5.9 %cholesky.16 = f32[64,64]{1,0:T(8,128)S(1)} custom-call(f32[64,64]{1,0:T(8,128)S(1)} %fusion.4), custom_call_target="Cholesky" | custom-call | tf_op jit(solution)/shard_map/jit(cholesky)/cholesky | solution.py:52
  136.8 0.6 compare_reduce_fusion
  137.5 0.7 fusion.2
  138.1 4.9 %custom-call.6 = f32[1,64,64]{1,2,0:T(8,128)S(1)} custom-call(f32[1,64,64]{2,1,0:T(8,128)S(1)} %fusion.2), custom_call_target="InvertDiagBlocksLowerTriangular" | custom-call | tf_op jit(solution)/shard_map/triangular_solve | solution.py:53
  143.0 1.0 fusion
  (2 shorter events, 0.0 us)
Async XLA Ops:
  0.0 1.0 copy-start
  0.0 8.4 %copy-start.1 = (bf16[4000,1536]{1,0:T(8,128)(2,1)S(1)}, bf16[4000,1536]{1,0:T(8,128)(2,1)}, u32[]{:S(2)}) copy-start(bf16[4000,1536]{1,0:T(8,128)(2,1)} %param.2) | copy-start | bytes 36864004
where the time goes:
time: 144 us
  blocking collectives  113 us (78%)
  other arithmetic  15.2 us (11%)
  matrix products  12.1 us (8%)
  local copies, waits for them, and re-layouts  3.42 us (2%)
    all_to_all x1, blocking collectives, copy_for_each(): lax.all_to_all(jnp.broadcast_to(array[None], (count, *array.shape)), axis...  71.6 us
    all_to_all x1, blocking collectives, summed_on_arrival(): lax.all_to_all(parts, axis, split_axis=0, concat_axis=0, tiled=True)  41.7 us
    dot_general x1, matrix products, on_device(): jnp.dot(sketch_map, expression, preferred_element_type=jnp.float32)  7.11 us
    another operation x3, other arithmetic, on_device(): lower = jnp.linalg.cholesky(gram)  6.53 us
    another operation x2, other arithmetic, on_device(): lax.linalg.triangular_solve(lower, own_genes, left_side=True, lower=True)  5.55 us
    dot_general x1, matrix products, on_device(): lax.dot_general(sketched, expression, (((1,), (1,)), ((), ())), preferred...  3.78 us

commit v1 on v0

v1 whole, which is shorter than its diff:
```python
import functools

import jax
import jax.numpy as jnp
from jax import lax
from jax.experimental import pallas as pl
from jax.experimental.pallas import tpu as pltpu
from jax.sharding import Mesh
from jax.sharding import PartitionSpec as P

WIDE = ("y", "x", "c")
CELL_BLOCK = 512
SPAN = 256


def nn(a, b):
    return lax.dot_general(a, b, (((1,), (0,)), ((), ())), preferred_element_type=jnp.float32)


def nt(a, b):
    return lax.dot_general(a, b, (((1,), (1,)), ((), ())), preferred_element_type=jnp.float32)


def front_kernel(parts, share, s_ref, e_ref, mine_ref, theirs_ref, acc, gram):
    step = pl.program_id(0)
    rows, genes = s_ref.shape

    @pl.when(step == 0)
    def _():
        acc[...] = jnp.zeros_like(acc)
        gram[...] = jnp.zeros_like(gram)

    block = e_ref[...]
    sketched = nn(s_ref[...], block).astype(jnp.bfloat16)
    gram[...] += nt(sketched, sketched)
    acc[:, :genes] += nt(sketched, block)

    @pl.when(step == pl.num_programs(0) - 1)
    def _():
        me = lax.axis_index("c")
        for ref, core in ((mine_ref, me), (theirs_ref, 1 - me)):
            packed = [
                gram[pl.ds(pl.multiple_of(16 * j + 8 * core, 8), 8), :] for j in range(rows // 16)
            ]
            packed = jnp.concatenate(packed, axis=1)
            for z in range(parts):
                start = z * share
                base, shift = start // 128 * 128, start % 128
                wide = acc[:, pl.ds(pl.multiple_of(base + SPAN * core, 128), SPAN + 128)]
                ref[z, :rows, :] = wide[:, shift : shift + SPAN]
                ref[z, rows:, :] = packed


def front(sketch_map, expression, parts):
    rows, genes = sketch_map.shape
    cells = expression.shape[1]
    out = jax.ShapeDtypeStruct((parts, rows + 8, SPAN), jnp.float32)
    whole = pl.BlockSpec(out.shape, lambda i: (0, 0, 0))
    return pl.pallas_call(
        functools.partial(front_kernel, parts, genes // parts),
        grid=(cells // CELL_BLOCK,),
        in_specs=[
            pl.BlockSpec((rows, genes), lambda i: (0, 0)),
            pl.BlockSpec((genes, CELL_BLOCK), lambda i: (0, i)),
        ],
        out_specs=[whole, whole],
        out_shape=[out, out],
        scratch_shapes=[
            pltpu.VMEM((rows, pl.cdiv(genes, 128) * 128), jnp.float32),
            pltpu.VMEM((rows, rows), jnp.float32),
        ],
        compiler_params=pltpu.CompilerParams(vmem_limit_bytes=48 << 20),
        name="front",
    )(sketch_map, expression)


def tail_kernel(share, mine_ref, other_ref, out_ref):
    me = lax.axis_index("c")
    rows = out_ref.shape[0]
    mine, other = mine_ref[...], other_ref[...]
    pair = [jnp.where(me == 0, mine, other), jnp.where(me == 0, other, mine)]
    sub = lax.broadcasted_iota(jnp.int32, (8, 128), 0)
    lane = lax.broadcasted_iota(jnp.int32, (8, 128), 1)
    work = []
    for g in range(rows // 8):
        held = pair[g % 2][rows:, 128 * (g // 4) : 128 * (g // 4) + 128]
        if (g // 2) % 2 == 0:
            held = pltpu.roll(held, 64, 1)
        work.append(jnp.where(lane < 64, jnp.where(lane == sub + 8 * g, 1.0, 0.0), held))
    pivots = [jnp.ones((8, 128), jnp.float32) for _ in work]
    for k in range(rows):
        group, s = k // 8, k % 8
        row = jnp.broadcast_to(work[group][s : s + 1, :], (8, 128))
        pivot = jnp.broadcast_to(row[:, 64 + k : 65 + k], (8, 128))
        pivots[group] = jnp.where(sub == s, pivot, pivots[group])
        scaled = row * (1.0 / pivot)
        for g in range(group, rows // 8):
            column = jnp.broadcast_to(work[g][:, 64 + k : 65 + k], (8, 128))
            if g == group:
                column = jnp.where(sub > s, column, 0.0)
            work[g] = work[g] - column * scaled
    inverse = [w * lax.rsqrt(p) for w, p in zip(work, pivots)]
    inverse = jnp.concatenate(inverse, axis=0)[:, :64]
    genes = jnp.concatenate([pair[0][:rows], pair[1][:rows]], axis=1)
    solved = lax.dot_general(
        inverse,
        genes,
        (((1,), (0,)), ((), ())),
        precision=lax.Precision.HIGHEST,
        preferred_element_type=jnp.float32,
    )
    out_ref[...] = solved[:, :share]


def tail(mine, other, rows, share):
    return pl.pallas_call(
        functools.partial(tail_kernel, share),
        in_specs=[pl.BlockSpec(memory_space=pltpu.VMEM)] * 2,
        out_specs=pl.BlockSpec(memory_space=pltpu.VMEM),
        out_shape=jax.ShapeDtypeStruct((rows, share), jnp.float32),
        name="tail",
    )(mine, other)


def wide_pairs(first, second):
    pairs = []
    for y in range(4):
        for x in range(4):
            for c, (ty, tx) in enumerate((first(y, x), second(y, x))):
                pairs.append(((y * 4 + x) * 2 + c, (ty * 4 + tx) * 2 + c))
    return pairs


def near(v):
    return v ^ 1


def across(v):
    return 3 - v


def on_device(expression, sketch_map):
    rows, genes = sketch_map.shape
    parts = lax.axis_size("z")
    mine, theirs = front(sketch_map, expression, parts)
    swap = [(0, 1), (1, 0)]
    summed = mine + lax.ppermute(theirs, "c", swap)
    total = lax.all_to_all(summed, "z", 0, 0, tiled=True).sum(axis=0)
    steps = (
        (lambda y, x: (y, near(x)), lambda y, x: (near(y), x)),
        (lambda y, x: (y, across(x)), lambda y, x: (across(y), x)),
        (lambda y, x: (near(y), x), lambda y, x: (y, near(x))),
        (lambda y, x: (across(y), x), lambda y, x: (y, across(x))),
    )
    for first, second in steps:
        total = total + lax.ppermute(total, WIDE, wide_pairs(first, second))
    other = lax.ppermute(total, "c", swap)
    return tail(total, other, rows, genes // parts)


def solution(mesh):
    grid = Mesh(mesh.devices.reshape(4, 4, 2, 8), ("y", "x", "c", "z"))
    placed = (P(None, ("y", "x", "c", "z")), P())
    return jax.shard_map(
        on_device, mesh=grid, in_specs=placed, out_specs=P(None, "z"), check_vma=False
    )
```

time: 144 us -> 73.2 us (0.51)
  blocking collectives: 113 us -> 24.6 us
  Pallas kernels: 0 us -> 18.8 us
  starting transfers between devices: 0 us -> 17.5 us
  other arithmetic: 15.2 us -> 0.16 us
  matrix products: 12.1 us -> 0 us
  waiting for transfers between devices: 0 us -> 10.1 us
  local copies, waits for them, and re-layouts: 3.42 us -> 1.68 us
    all_to_all x2 -> x1, blocking collectives: 113 us -> 24.6 us  [on_device(): total = lax.all_to_all(summed, 'z', 0, 0, tiled=True).sum(axis=0)]
    pallas_call x0 -> x2, Pallas kernels: none -> 18.8 us  [the longest x1 10.2 us: tail(): pl.pallas_call(functools.partial(tail_kernel, share), in_specs=[pl.BlockS...]
    ppermute x0 -> x6, starting transfers between devices: none -> 17.5 us  [the longest x4 8.07 us: on_device(): total = total + lax.ppermute(total, WIDE, wide_pairs(first, second))]
    another operation x5 -> x0, other arithmetic: 12.1 us -> none  [the longest x3 6.53 us: on_device(): lower = jnp.linalg.cholesky(gram)]
    dot_general x3 -> x0, matrix products: 11.1 us -> none  [the longest x1 7.11 us: on_device(): jnp.dot(sketch_map, expression, preferred_element_type=jnp.float32)]
    ppermute x0 -> x6, waiting for transfers between devices: none -> 10.1 us  [the longest x4 7.58 us: on_device(): total = total + lax.ppermute(total, WIDE, wide_pairs(first, second))]
    reduce_sum x2 -> x1, other arithmetic: 2.85 us -> 0.04 us  [on_device(): total = lax.all_to_all(summed, 'z', 0, 0, tiled=True).sum(axis=0)]
    reshape x2 -> x0, local copies, waits for them, and re-layouts: 1.62 us -> none  [on_device(): blocks = products.reshape(rows_count, group_count, share_width)]
  transfers between devices with their start and end apart: 0 -> 6, of which waited for: 0 -> 6; matrix products, arithmetic and copies ran while one was open for 0% -> 0% of each run, Pallas kernels for 0% -> 0%
where the time goes in v1:
time: 73.2 us; the launch traced here: 73 us
  blocking collectives  24.6 us (34%)
  Pallas kernels  18.8 us (26%)
  starting transfers between devices  17.5 us (24%)
  waiting for transfers between devices  10.1 us (14%)
  local copies, waits for them, and re-layouts  1.68 us (2%)
    all_to_all x1, blocking collectives, on_device(): total = lax.all_to_all(summed, 'z', 0, 0, tiled=True).sum(axis=0)  24.6 us
    pallas_call x1, Pallas kernels, tail(): pl.pallas_call(functools.partial(tail_kernel, share), in_specs=[pl.BlockS...  10.2 us
    pallas_call x1, Pallas kernels, front(): pl.pallas_call(functools.partial(front_kernel, parts, genes // parts), gr...  8.63 us
    ppermute x4, starting transfers between devices, on_device(): total = total + lax.ppermute(total, WIDE, wide_pairs(first, second))  8.07 us
    ppermute x4, waiting for transfers between devices, on_device(): total = total + lax.ppermute(total, WIDE, wide_pairs(first, second))  7.58 us
    ppermute x1, starting transfers between devices, on_device(): other = lax.ppermute(total, 'c', swap)  6.07 us
    ppermute x1, starting transfers between devices, on_device(): summed = mine + lax.ppermute(theirs, 'c', swap)  3.33 us
    unnamed x6, local copies, waits for them, and re-layouts  1.68 us
  transfers between devices with their start and end apart: 6, of which 6 were waited for; matrix products, arithmetic and copies ran while one was open for 0% of the time, Pallas kernels for 0%

profile of v1, /device:TPU:1, one launch (start us, length us, event | category | flops | bytes accessed | tf_op | source)
XLA Modules:
  0.0 73.0 jit_solution(16480586923956201080)
XLA Ops:
  0.0 0.0 copy-start
  0.0 1.0 %copy-done = bf16[64,4000]{1,0:T(8,128)(2,1)S(1)} copy-done((bf16[64,4000]{1,0:T(8,128)(2,1)S(1)}, bf16[64,4000]{1,0:T(8,128)(2,1)}, u32[]{:S(2)}) %copy-start) | copy-done | bytes 512024
  1.0 8.6 %front.1 = (f32[8,72,256]{2,1,0:T(8,128)S(1)}, f32[8,72,256]{2,1,0:T(8,128)S(1)}) custom-call(bf16[64,4000]{1,0:T(8,128)(2,1)S(1)} %copy-done, bf16[4000,1536]{1,0:T(8,128)(2,1)} %e_ref.1), custom_call_target="tpu_custom_call" | custom-call | tf_op jit(solution)/shard_map/front/pallas_call | solution.py:59
  9.7 3.3 %collective-permute-start = (f32[8,72,256]{2,1,0:T(8,128)S(1)}, f32[8,72,256]{2,1,0:T(8,128)S(1)}, u32[]{:S(2)}, u32[]{:S(2)}) collective-permute-start(f32[8,72,256]{2,1,0:T(8,128)S(1)} %get-tuple-element.8), channel_id=1, source_target_pairs={{0,8},{8,0},{1,9},{9,1},{2,10},{10,2},{3,11},{11,3},{4,12},{12,4},... | collective-permute-start | bytes 1769480 | tf_op jit(solution)/shard_map/ppermute | solution.py:147
  13.0 1.6 %collective-permute-done = f32[8,72,256]{2,1,0:T(8,128)S(1)} collective-permute-done((f32[8,72,256]{2,1,0:T(8,128)S(1)}, f32[8,72,256]{2,1,0:T(8,128)S(1)}, u32[]{:S(2)}, u32[]{:S(2)}) %collective-permute-start) | collective-permute-done | bytes 589856 | tf_op jit(solution)/shard_map/ppermute | solution.py:147
  14.6 0.1 add.15
  14.7 24.6 %all_to_all.5 = f32[8,72,256]{2,1,0:T(8,128)S(1)} all-to-all(f32[8,72,256]{2,1,0:T(8,128)S(1)} %add.15), channel_id=1, replica_groups=mesh['y'=4,'x'=4,'c'=2,'z'=8] {'z'}, dimensions={0} | all-to-all | bytes 1179648 | tf_op jit(solution)/shard_map/all_to_all | solution.py:148
  39.4 1.4 %collective-permute-start.1 = (f32[72,256]{1,0:T(8,128)S(1)}, f32[72,256]{1,0:T(8,128)S(1)}, u32[]{:S(2)}, u32[]{:S(2)}) collective-permute-start(f32[72,256]{1,0:T(8,128)S(1)} %reduce_sum.9), channel_id=1, source_target_pairs={{0,16},{8,72},{16,0},{24,88},{32,48},{40,104},{48,32},{56,120},{64... | collective-permute-start | bytes 221192 | tf_op jit(solution)/shard_map/ppermute | solution.py:156
  40.8 1.9 %collective-permute-done.1 = f32[72,256]{1,0:T(8,128)S(1)} collective-permute-done((f32[72,256]{1,0:T(8,128)S(1)}, f32[72,256]{1,0:T(8,128)S(1)}, u32[]{:S(2)}, u32[]{:S(2)}) %collective-permute-start.1) | collective-permute-done | bytes 73760 | tf_op jit(solution)/shard_map/ppermute | solution.py:156
  42.7 2.8 %collective-permute-start.2 = (f32[72,256]{1,0:T(8,128)S(1)}, f32[72,256]{1,0:T(8,128)S(1)}, u32[]{:S(2)}, u32[]{:S(2)}) collective-permute-start(f32[72,256]{1,0:T(8,128)S(1)} %add.16), channel_id=1, source_target_pairs={{0,48},{8,200},{16,32},{24,216},{32,16},{40,232},{48,0},{56,248},{... | collective-permute-start | bytes 221192 | tf_op jit(solution)/shard_map/ppermute | solution.py:156
  45.5 1.7 %collective-permute-done.2 = f32[72,256]{1,0:T(8,128)S(1)} collective-permute-done((f32[72,256]{1,0:T(8,128)S(1)}, f32[72,256]{1,0:T(8,128)S(1)}, u32[]{:S(2)}, u32[]{:S(2)}) %collective-permute-start.2) | collective-permute-done | bytes 73760 | tf_op jit(solution)/shard_map/ppermute | solution.py:156
  47.3 1.3 %collective-permute-start.3 = (f32[72,256]{1,0:T(8,128)S(1)}, f32[72,256]{1,0:T(8,128)S(1)}, u32[]{:S(2)}, u32[]{:S(2)}) collective-permute-start(f32[72,256]{1,0:T(8,128)S(1)} %add.17), channel_id=1, source_target_pairs={{0,64},{8,24},{16,80},{24,8},{32,96},{40,56},{48,112},{56,40},{64,... | collective-permute-start | bytes 221192 | tf_op jit(solution)/shard_map/ppermute | solution.py:156
  48.6 2.0 %collective-permute-done.3 = f32[72,256]{1,0:T(8,128)S(1)} collective-permute-done((f32[72,256]{1,0:T(8,128)S(1)}, f32[72,256]{1,0:T(8,128)S(1)}, u32[]{:S(2)}, u32[]{:S(2)}) %collective-permute-start.3) | collective-permute-done | bytes 73760 | tf_op jit(solution)/shard_map/ppermute | solution.py:156
  50.6 2.6 %collective-permute-start.4 = (f32[72,256]{1,0:T(8,128)S(1)}, f32[72,256]{1,0:T(8,128)S(1)}, u32[]{:S(2)}, u32[]{:S(2)}) collective-permute-start(f32[72,256]{1,0:T(8,128)S(1)} %add.18), channel_id=1, source_target_pairs={{0,192},{8,56},{16,208},{24,40},{32,224},{40,24},{48,240},{56,8},{... | collective-permute-start | bytes 221192 | tf_op jit(solution)/shard_map/ppermute | solution.py:156
  53.2 1.9 %collective-permute-done.4 = f32[72,256]{1,0:T(8,128)S(1)} collective-permute-done((f32[72,256]{1,0:T(8,128)S(1)}, f32[72,256]{1,0:T(8,128)S(1)}, u32[]{:S(2)}, u32[]{:S(2)}) %collective-permute-start.4) | collective-permute-done | bytes 73760 | tf_op jit(solution)/shard_map/ppermute | solution.py:156
  55.1 0.0 copy-start.1
  55.1 6.1 %collective-permute-start.5 = (f32[72,256]{1,0:T(8,128)S(1)}, f32[72,256]{1,0:T(8,128)S(1)}, u32[]{:S(2)}, u32[]{:S(2)}) collective-permute-start(f32[72,256]{1,0:T(8,128)S(1)} %add.19.mine_ref), channel_id=1, source_target_pairs={{0,8},{8,0},{1,9},{9,1},{2,10},{10,2},{3,11},{11,3},{4,12},{12,4},... | collective-permute-start | bytes 221192 | tf_op jit(solution)/shard_map/ppermute | solution.py:157
  61.2 0.9 %collective-permute-done.5.other_ref = f32[72,256]{1,0:T(8,128)S(1)} collective-permute-done((f32[72,256]{1,0:T(8,128)S(1)}, f32[72,256]{1,0:T(8,128)S(1)}, u32[]{:S(2)}, u32[]{:S(2)}) %collective-permute-start.5) | collective-permute-done | bytes 73760 | tf_op jit(solution)/shard_map/ppermute | solution.py:157
  62.1 0.0 copy-done.1
  62.1 0.0 copy-start.2
  62.1 0.6 copy-done.2
  62.8 10.2 %tail.1 = f32[64,500]{1,0:T(8,128)} custom-call(f32[72,256]{1,0:T(8,128)} %copy-done.1, f32[72,256]{1,0:T(8,128)} %copy-done.2), custom_call_target="tpu_custom_call" | custom-call | tf_op jit(solution)/shard_map/tail/pallas_call | solution.py:116
  (5 shorter events, 0.1 us)
Async XLA Ops:
  0.0 1.0 %copy-start = (bf16[64,4000]{1,0:T(8,128)(2,1)S(1)}, bf16[64,4000]{1,0:T(8,128)(2,1)}, u32[]{:S(2)}) copy-start(bf16[64,4000]{1,0:T(8,128)(2,1)} %s_ref.1) | copy-start | bytes 1536004
  9.7 5.0 %collective-permute-start = (f32[8,72,256]{2,1,0:T(8,128)S(1)}, f32[8,72,256]{2,1,0:T(8,128)S(1)}, u32[]{:S(2)}, u32[]{:S(2)}) collective-permute-start(f32[8,72,256]{2,1,0:T(8,128)S(1)} %get-tuple-element.8), channel_id=1, source_target_pairs={{0,8},{8,0},{1,9},{9,1},{2,10},{10,2},{3,11},{11,3},{4,12},{12,4},... | collective-permute-start | bytes 1769480 | tf_op jit(solution)/shard_map/ppermute | solution.py:147
  39.4 3.3 %collective-permute-start.1 = (f32[72,256]{1,0:T(8,128)S(1)}, f32[72,256]{1,0:T(8,128)S(1)}, u32[]{:S(2)}, u32[]{:S(2)}) collective-permute-start(f32[72,256]{1,0:T(8,128)S(1)} %reduce_sum.9), channel_id=1, source_target_pairs={{0,16},{8,72},{16,0},{24,88},{32,48},{40,104},{48,32},{56,120},{64... | collective-permute-start | bytes 221192 | tf_op jit(solution)/shard_map/ppermute | solution.py:156
  42.7 4.6 %collective-permute-start.2 = (f32[72,256]{1,0:T(8,128)S(1)}, f32[72,256]{1,0:T(8,128)S(1)}, u32[]{:S(2)}, u32[]{:S(2)}) collective-permute-start(f32[72,256]{1,0:T(8,128)S(1)} %add.16), channel_id=1, source_target_pairs={{0,48},{8,200},{16,32},{24,216},{32,16},{40,232},{48,0},{56,248},{... | collective-permute-start | bytes 221192 | tf_op jit(solution)/shard_map/ppermute | solution.py:156
  47.3 3.3 %collective-permute-start.3 = (f32[72,256]{1,0:T(8,128)S(1)}, f32[72,256]{1,0:T(8,128)S(1)}, u32[]{:S(2)}, u32[]{:S(2)}) collective-permute-start(f32[72,256]{1,0:T(8,128)S(1)} %add.17), channel_id=1, source_target_pairs={{0,64},{8,24},{16,80},{24,8},{32,96},{40,56},{48,112},{56,40},{64,... | collective-permute-start | bytes 221192 | tf_op jit(solution)/shard_map/ppermute | solution.py:156
  50.6 4.5 %collective-permute-start.4 = (f32[72,256]{1,0:T(8,128)S(1)}, f32[72,256]{1,0:T(8,128)S(1)}, u32[]{:S(2)}, u32[]{:S(2)}) collective-permute-start(f32[72,256]{1,0:T(8,128)S(1)} %add.18), channel_id=1, source_target_pairs={{0,192},{8,56},{16,208},{24,40},{32,224},{40,24},{48,240},{56,8},{... | collective-permute-start | bytes 221192 | tf_op jit(solution)/shard_map/ppermute | solution.py:156
  55.1 7.0 %copy-start.1 = (f32[72,256]{1,0:T(8,128)}, f32[72,256]{1,0:T(8,128)S(1)}, u32[]{:S(2)}) copy-start(f32[72,256]{1,0:T(8,128)S(1)} %add.19.mine_ref) | copy-start | bytes 221188
  55.1 7.0 %collective-permute-start.5 = (f32[72,256]{1,0:T(8,128)S(1)}, f32[72,256]{1,0:T(8,128)S(1)}, u32[]{:S(2)}, u32[]{:S(2)}) collective-permute-start(f32[72,256]{1,0:T(8,128)S(1)} %add.19.mine_ref), channel_id=1, source_target_pairs={{0,8},{8,0},{1,9},{9,1},{2,10},{10,2},{3,11},{11,3},{4,12},{12,4},... | collective-permute-start | bytes 221192 | tf_op jit(solution)/shard_map/ppermute | solution.py:157
  62.1 0.6 copy-start.2

commit v2 on v0

v2 whole, which is shorter than its diff:
```python
import functools

import jax
import jax.numpy as jnp
from jax import lax
from jax.experimental import pallas as pl
from jax.experimental.pallas import tpu as pltpu
from jax.sharding import Mesh
from jax.sharding import PartitionSpec as P

WIDE = ("y", "x", "c")
CHUNKS = (512, 512, 512)
SPAN = 256


def nn(a, b):
    return lax.dot_general(a, b, (((1,), (0,)), ((), ())), preferred_element_type=jnp.float32)


def nt(a, b):
    return lax.dot_general(a, b, (((1,), (1,)), ((), ())), preferred_element_type=jnp.float32)


def front_kernel(parts, share, s_hbm, e_hbm, mine_ref, theirs_ref, s_ref, *scratch):
    count = len(CHUNKS)
    blocks = scratch[:count]
    acc, gram, sems = scratch[count:]
    rows, genes = s_ref.shape
    copies = [pltpu.make_async_copy(s_hbm, s_ref, sems.at[count])]
    start = 0
    for i, size in enumerate(CHUNKS):
        copies.append(
            pltpu.make_async_copy(e_hbm.at[:, pl.ds(start, size)], blocks[i], sems.at[i])
        )
        start += size
    for copy in copies:
        copy.start()
    acc[:, genes:] = jnp.zeros((rows, acc.shape[1] - genes), jnp.float32)
    copies[0].wait()
    total = None
    for i in range(count):
        copies[i + 1].wait()
        block = blocks[i][...]
        sketched = nn(s_ref[...], block).astype(jnp.bfloat16)
        square = nt(sketched, sketched)
        total = square if i == 0 else total + square
        if i == 0:
            acc[:, :genes] = nt(sketched, block)
        else:
            acc[:, :genes] += nt(sketched, block)
    half = rows // 2
    gram[...] = jnp.concatenate([total[:half], total[half:]], axis=1)
    me = lax.axis_index("c")
    for ref, core in ((mine_ref, me), (theirs_ref, 1 - me)):
        for z in range(parts):
            base, shift = z * share // 128 * 128, z * share % 128
            wide = acc[:, pl.ds(pl.multiple_of(base + SPAN * core, 128), SPAN + 128)]
            part = wide[:, shift : shift + SPAN]
            for m in range(rows // 4):
                r, c = m // 2 * 8, m % 2 * 128
                ref[m, 8 * z : 8 * z + 8, :] = part[r : r + 8, c : c + 128]
        for m in range(rows // 4):
            row = gram[pl.ds(2 * m + core, 1), :]
            ref[m, 8 * parts :, :] = jnp.broadcast_to(row, (8, 128))


def front(sketch_map, expression, parts):
    rows, genes = sketch_map.shape
    out = jax.ShapeDtypeStruct((rows // 4, 8 * parts + 8, 128), jnp.float32)
    return pl.pallas_call(
        functools.partial(front_kernel, parts, genes // parts),
        in_specs=[pl.BlockSpec(memory_space=pltpu.HBM)] * 2,
        out_specs=[pl.BlockSpec(memory_space=pltpu.VMEM)] * 2,
        out_shape=[out, out],
        scratch_shapes=[pltpu.VMEM((rows, genes), jnp.bfloat16)]
        + [pltpu.VMEM((genes, size), jnp.bfloat16) for size in CHUNKS]
        + [
            pltpu.VMEM((rows, pl.cdiv(genes, 128) * 128), jnp.float32),
            pltpu.VMEM((rows // 2, 2 * rows), jnp.float32),
            pltpu.SemaphoreType.DMA((len(CHUNKS) + 1,)),
        ],
        compiler_params=pltpu.CompilerParams(vmem_limit_bytes=40 << 20),
        name="front",
    )(
        pltpu.with_memory_space_constraint(sketch_map, pltpu.HBM),
        pltpu.with_memory_space_constraint(expression, pltpu.HBM),
    )


def added(ref, where):
    parts = [ref[i, where, :] for i in range(ref.shape[0])]
    while len(parts) > 1:
        parts = [a + b for a, b in zip(parts[::2], parts[1::2])]
    return parts[0]


def spread_kernel(in_ref, out_ref):
    parts = out_ref.shape[0]
    square = added(in_ref, slice(8 * parts, 8 * parts + 8))
    for z in range(parts):
        out_ref[z, :8, :] = added(in_ref, slice(8 * z, 8 * z + 8))
        out_ref[z, 8:, :] = square


def repeat_kernel(in_ref, out_ref):
    whole = added(in_ref, slice(None))
    for i in range(out_ref.shape[0]):
        out_ref[i] = whole


def small(kernel, shape, name, *args):
    return pl.pallas_call(
        kernel,
        in_specs=[pl.BlockSpec(memory_space=pltpu.VMEM)] * len(args),
        out_specs=pl.BlockSpec(memory_space=pltpu.VMEM),
        out_shape=jax.ShapeDtypeStruct(shape, jnp.float32),
        name=name,
    )(*args)


def over_tile(x):
    return jnp.broadcast_to(x, (8, 128))


def inverse_factor(work, sub):
    count = len(work)
    for g in range(count):
        block = work[g]
        at = 64 + 8 * g
        columns = [over_tile(block[:, at + j : at + j + 1]) for j in range(8)]
        a = {(i, j): over_tile(columns[j][i : i + 1]) for j in range(8) for i in range(j, 8)}
        rows = [over_tile(block[i : i + 1]) for i in range(8)]
        low, inverse = {}, []
        for j in range(8):
            inverse.append(1.0 / a[j, j])
            for i in range(j + 1, 8):
                low[i, j] = a[i, j] * inverse[j]
            for i in range(j + 1, 8):
                for m in range(j + 1, i + 1):
                    a[i, m] = a[i, m] - low[i, j] * a[m, j]
        solved = []
        for i in range(8):
            row = rows[i]
            for j in range(i):
                row = row - low[i, j] * solved[j]
            solved.append(row)
        if g < count - 1:
            back = [None] * 8
            for i in reversed(range(8)):
                row = solved[i] * inverse[i]
                for j in range(i + 1, 8):
                    row = row - low[j, i] * back[j]
                back[i] = row
            for h in range(g + 1, count):
                left = work[h]
                for j in range(8):
                    left = left - over_tile(work[h][:, at + j : at + j + 1]) * back[j]
                work[h] = left
        block, pivots = solved[0], a[0, 0]
        for i in range(1, 8):
            block = jnp.where(sub == i, solved[i], block)
            pivots = jnp.where(sub == i, a[i, i], pivots)
        work[g] = block * lax.rsqrt(pivots)
    return work


def tail_kernel(in_ref, out_ref):
    rows, share = out_ref.shape
    sub = lax.broadcasted_iota(jnp.int32, (8, 128), 0)
    lane = lax.broadcasted_iota(jnp.int32, (8, 128), 1)
    gram = in_ref[:, 8, :]
    work = []
    for g in range(rows // 8):
        held = gram[8 * (g % 4) : 8 * (g % 4) + 8]
        if g < 4:
            held = pltpu.roll(held, 64, 1)
        work.append(jnp.where(lane < 64, jnp.where(lane == sub + 8 * g, 1.0, 0.0), held))
    inverse = jnp.concatenate(inverse_factor(work, sub), axis=0)[:, :rows]
    genes = jnp.concatenate(
        [
            jnp.concatenate([in_ref[(2 * r + h) * 2 + c, :8, :] for r in range(rows // 8)], axis=0)
            for c in range(2)
            for h in range(2)
        ],
        axis=1,
    )
    solved = lax.dot_general(
        inverse,
        genes,
        (((1,), (0,)), ((), ())),
        precision=lax.Precision.HIGHEST,
        preferred_element_type=jnp.float32,
    )
    out_ref[...] = solved[:, :share]


def on_device(expression, sketch_map):
    rows, genes = sketch_map.shape
    parts = lax.axis_size("z")
    mine, theirs = front(sketch_map, expression, parts)
    summed = mine + lax.ppermute(theirs, "c", [(0, 1), (1, 0)])
    arrived = lax.all_to_all(summed, ("y", "x"), 0, 0, tiled=True)
    piece = small(spread_kernel, (parts, 16, 128), "spread", arrived)
    arrived = lax.all_to_all(piece, "z", 0, 0, tiled=True)
    piece = small(repeat_kernel, (lax.axis_size(WIDE), 16, 128), "repeat", arrived)
    arrived = lax.all_to_all(piece, WIDE, 0, 0, tiled=True)
    return small(tail_kernel, (rows, genes // parts), "tail", arrived)


def solution(mesh):
    grid = Mesh(mesh.devices.reshape(4, 4, 2, 8), ("y", "x", "c", "z"))
    placed = (P(None, ("y", "x", "c", "z")), P())
    return jax.shard_map(
        on_device, mesh=grid, in_specs=placed, out_specs=P(None, "z"), check_vma=False
    )
```

time: 144 us -> 70.2 us (0.49)
  blocking collectives: 113 us -> 48.3 us
  Pallas kernels: 0 us -> 16.5 us
  other arithmetic: 15.2 us -> 0.06 us
  matrix products: 12.1 us -> 0 us
  local copies, waits for them, and re-layouts: 3.42 us -> 0 us
  starting transfers between devices: 0 us -> 3.32 us
  waiting for transfers between devices: 0 us -> 1.63 us
    all_to_all x2 -> x3, blocking collectives: 113 us -> 48.3 us  [the longest x1 16.5 us: on_device(): arrived = lax.all_to_all(piece, WIDE, 0, 0, tiled=True)]
    pallas_call x0 -> x4, Pallas kernels: none -> 16.5 us  [the longest x1 8.82 us: front(): pl.pallas_call(functools.partial(front_kernel, parts, genes // parts), in...]
    another operation x5 -> x0, other arithmetic: 12.1 us -> none  [the longest x3 6.53 us: on_device(): lower = jnp.linalg.cholesky(gram)]
    dot_general x3 -> x0, matrix products: 11.1 us -> none  [the longest x1 7.11 us: on_device(): jnp.dot(sketch_map, expression, preferred_element_type=jnp.float32)]
    ppermute x0 -> x1, starting transfers between devices: none -> 3.32 us  [on_device(): summed = mine + lax.ppermute(theirs, 'c', [(0, 1), (1, 0)])]
    reduce_sum x2 -> x0, other arithmetic: 2.85 us -> none  [the longest x1 2.77 us: taken_together(): return copy_for_each(array, axis).sum(axis=0)]
    ppermute x0 -> x1, waiting for transfers between devices: none -> 1.63 us  [on_device(): summed = mine + lax.ppermute(theirs, 'c', [(0, 1), (1, 0)])]
    reshape x2 -> x0, local copies, waits for them, and re-layouts: 1.62 us -> none  [on_device(): blocks = products.reshape(rows_count, group_count, share_width)]
  transfers between devices with their start and end apart: 0 -> 1, of which waited for: 0 -> 1; matrix products, arithmetic and copies ran while one was open for 0% -> 0% of each run, Pallas kernels for 0% -> 0%
where the time goes in v2:
time: 70.2 us; the launch traced here: 69.9 us
  blocking collectives  48.3 us (69%)
  Pallas kernels  16.5 us (24%)
  starting transfers between devices  3.32 us (5%)
  waiting for transfers between devices  1.63 us (2%)
    all_to_all x1, blocking collectives, on_device(): arrived = lax.all_to_all(piece, WIDE, 0, 0, tiled=True)  16.5 us
    all_to_all x1, blocking collectives, on_device(): arrived = lax.all_to_all(summed, ('y', 'x'), 0, 0, tiled=True)  16.3 us
    all_to_all x1, blocking collectives, on_device(): arrived = lax.all_to_all(piece, 'z', 0, 0, tiled=True)  15.5 us
    pallas_call x1, Pallas kernels, front(): pl.pallas_call(functools.partial(front_kernel, parts, genes // parts), in...  8.82 us
    pallas_call x3, Pallas kernels, small(): pl.pallas_call(kernel, in_specs=[pl.BlockSpec(memory_space=pltpu.VMEM)] *...  7.7 us
    ppermute x1, starting transfers between devices, on_device(): summed = mine + lax.ppermute(theirs, 'c', [(0, 1), (1, 0)])  3.32 us
    ppermute x1, waiting for transfers between devices, on_device(): summed = mine + lax.ppermute(theirs, 'c', [(0, 1), (1, 0)])  1.63 us
  transfers between devices with their start and end apart: 1, of which 1 were waited for; matrix products, arithmetic and copies ran while one was open for 0% of the time, Pallas kernels for 0%

profile of v2, /device:TPU:1, one launch (start us, length us, event | category | flops | bytes accessed | tf_op | source)
XLA Modules:
  0.0 69.9 jit_solution(4123898698136755473)
XLA Ops:
  0.0 8.8 %front.1 = (f32[16,72,128]{2,1,0:T(8,128)S(1)}, f32[16,72,128]{2,1,0:T(8,128)S(1)}) custom-call(bf16[64,4000]{1,0:T(8,128)(2,1)} %s_hbm.1, bf16[4000,1536]{1,0:T(8,128)(2,1)} %e_hbm.1), custom_call_target="tpu_custom_call" | custom-call | tf_op jit(solution)/shard_map/front/pallas_call | solution.py:70
  8.8 3.3 %collective-permute-start = (f32[16,72,128]{2,1,0:T(8,128)S(1)}, f32[16,72,128]{2,1,0:T(8,128)S(1)}, u32[]{:S(2)}, u32[]{:S(2)}) collective-permute-start(f32[16,72,128]{2,1,0:T(8,128)S(1)} %get-tuple-element.8), channel_id=1, source_target_pairs={{0,8},{8,0},{1,9},{9,1},{2,10},{10,2},{3,11},{11,3},{4,12},{12,4},... | collective-permute-start | bytes 1769480 | tf_op jit(solution)/shard_map/ppermute | solution.py:201
  12.2 1.6 %collective-permute-done = f32[16,72,128]{2,1,0:T(8,128)S(1)} collective-permute-done((f32[16,72,128]{2,1,0:T(8,128)S(1)}, f32[16,72,128]{2,1,0:T(8,128)S(1)}, u32[]{:S(2)}, u32[]{:S(2)}) %collective-permute-start) | collective-permute-done | bytes 589856 | tf_op jit(solution)/shard_map/ppermute | solution.py:201
  13.8 0.1 add.3
  13.8 16.3 %all_to_all.15.in_ref = f32[16,72,128]{2,1,0:T(8,128)} all-to-all(f32[16,72,128]{2,1,0:T(8,128)S(1)} %add.3), channel_id=1, replica_groups=mesh['y'=4,'x'=4,'c'=2,'z'=8] {'y','x'}, dimensions={0} | all-to-all | bytes 1179648 | tf_op jit(solution)/shard_map/all_to_all | solution.py:202
  30.2 1.7 %spread.1 = f32[8,16,128]{2,1,0:T(8,128)} custom-call(f32[16,72,128]{2,1,0:T(8,128)} %all_to_all.15.in_ref), custom_call_target="tpu_custom_call" | custom-call | tf_op jit(solution)/shard_map/spread/pallas_call | solution.py:112
  31.9 15.5 %all_to_all.16.in_ref = f32[8,16,128]{2,1,0:T(8,128)} all-to-all(f32[8,16,128]{2,1,0:T(8,128)} %spread.1), channel_id=1, replica_groups=mesh['y'=4,'x'=4,'c'=2,'z'=8] {'z'}, dimensions={0} | all-to-all | bytes 131072 | tf_op jit(solution)/shard_map/all_to_all | solution.py:204
  47.4 1.5 %repeat.1 = f32[32,16,128]{2,1,0:T(8,128)} custom-call(f32[8,16,128]{2,1,0:T(8,128)} %all_to_all.16.in_ref), custom_call_target="tpu_custom_call" | custom-call | tf_op jit(solution)/shard_map/repeat/pallas_call | solution.py:112
  49.0 16.5 %all_to_all.17.in_ref = f32[32,16,128]{2,1,0:T(8,128)} all-to-all(f32[32,16,128]{2,1,0:T(8,128)} %repeat.1), channel_id=1, replica_groups=mesh['y'=4,'x'=4,'c'=2,'z'=8] {'y','x','c'}, dimensions={0} | all-to-all | bytes 524288 | tf_op jit(solution)/shard_map/all_to_all | solution.py:206
  65.4 4.4 %tail.1 = f32[64,500]{1,0:T(8,128)} custom-call(f32[32,16,128]{2,1,0:T(8,128)} %all_to_all.17.in_ref), custom_call_target="tpu_custom_call" | custom-call | tf_op jit(solution)/shard_map/tail/pallas_call | solution.py:112
Async XLA Ops:
  8.8 5.0 %collective-permute-start = (f32[16,72,128]{2,1,0:T(8,128)S(1)}, f32[16,72,128]{2,1,0:T(8,128)S(1)}, u32[]{:S(2)}, u32[]{:S(2)}) collective-permute-start(f32[16,72,128]{2,1,0:T(8,128)S(1)} %get-tuple-element.8), channel_id=1, source_target_pairs={{0,8},{8,0},{1,9},{9,1},{2,10},{10,2},{3,11},{11,3},{4,12},{12,4},... | collective-permute-start | bytes 1769480 | tf_op jit(solution)/shard_map/ppermute | solution.py:201

commit v3 on v2

--- a/solution.py
+++ b/solution.py
@@ -48,8 +48,11 @@
             acc[:, :genes] = nt(sketched, block)
         else:
             acc[:, :genes] += nt(sketched, block)
-    half = rows // 2
-    gram[...] = jnp.concatenate([total[:half], total[half:]], axis=1)
+    quarter = rows // 4
+    for h in range(2):
+        top = total[2 * quarter * h : 2 * quarter * h + quarter]
+        low = total[2 * quarter * h + quarter : 2 * quarter * (h + 1)]
+        gram[quarter * h : quarter * (h + 1), :] = jnp.concatenate([top, low], axis=1)
     me = lax.axis_index("c")
     for ref, core in ((mine_ref, me), (theirs_ref, 1 - me)):
         for z in range(parts):
@@ -59,14 +62,14 @@
             for m in range(rows // 4):
                 r, c = m // 2 * 8, m % 2 * 128
                 ref[m, 8 * z : 8 * z + 8, :] = part[r : r + 8, c : c + 128]
-        for m in range(rows // 4):
-            row = gram[pl.ds(2 * m + core, 1), :]
-            ref[m, 8 * parts :, :] = jnp.broadcast_to(row, (8, 128))
+        half = gram[pl.ds(pl.multiple_of(quarter * core, 8), quarter), :]
+        for m in range(quarter):
+            ref[m, 8 * parts :, :] = half
 
 
 def front(sketch_map, expression, parts):
     rows, genes = sketch_map.shape
-    out = jax.ShapeDtypeStruct((rows // 4, 8 * parts + 8, 128), jnp.float32)
+    out = jax.ShapeDtypeStruct((rows // 4, 8 * parts + rows // 4, 128), jnp.float32)
     return pl.pallas_call(
         functools.partial(front_kernel, parts, genes // parts),
         in_specs=[pl.BlockSpec(memory_space=pltpu.HBM)] * 2,
@@ -85,27 +88,6 @@
         pltpu.with_memory_space_constraint(sketch_map, pltpu.HBM),
         pltpu.with_memory_space_constraint(expression, pltpu.HBM),
     )
-
-
-def added(ref, where):
-    parts = [ref[i, where, :] for i in range(ref.shape[0])]
-    while len(parts) > 1:
-        parts = [a + b for a, b in zip(parts[::2], parts[1::2])]
-    return parts[0]
-
-
-def spread_kernel(in_ref, out_ref):
-    parts = out_ref.shape[0]
-    square = added(in_ref, slice(8 * parts, 8 * parts + 8))
-    for z in range(parts):
-        out_ref[z, :8, :] = added(in_ref, slice(8 * z, 8 * z + 8))
-        out_ref[z, 8:, :] = square
-
-
-def repeat_kernel(in_ref, out_ref):
-    whole = added(in_ref, slice(None))
-    for i in range(out_ref.shape[0]):
-        out_ref[i] = whole
 
 
 def small(kernel, shape, name, *args):
@@ -164,28 +146,34 @@
     return work
 
 
-def tail_kernel(in_ref, out_ref):
-    rows, share = out_ref.shape
+def factor_kernel(mine_ref, other_ref, out_ref):
+    me = lax.axis_index("c")
+    mine, other = mine_ref[...], other_ref[...]
+    halves = [jnp.where(me == 0, mine, other), jnp.where(me == 0, other, mine)]
     sub = lax.broadcasted_iota(jnp.int32, (8, 128), 0)
     lane = lax.broadcasted_iota(jnp.int32, (8, 128), 1)
-    gram = in_ref[:, 8, :]
     work = []
-    for g in range(rows // 8):
-        held = gram[8 * (g % 4) : 8 * (g % 4) + 8]
-        if g < 4:
+    for g in range(8):
+        held = halves[g // 4][8 * (g % 2) : 8 * (g % 2) + 8]
+        if g // 2 % 2 == 0:
             held = pltpu.roll(held, 64, 1)
         work.append(jnp.where(lane < 64, jnp.where(lane == sub + 8 * g, 1.0, 0.0), held))
-    inverse = jnp.concatenate(inverse_factor(work, sub), axis=0)[:, :rows]
+    for g, block in enumerate(inverse_factor(work, sub)):
+        out_ref[8 * g : 8 * g + 8, :] = block[:, :64]
+
+
+def apply_kernel(inverse_ref, in_ref, out_ref):
+    rows, share = out_ref.shape
     genes = jnp.concatenate(
         [
-            jnp.concatenate([in_ref[(2 * r + h) * 2 + c, :8, :] for r in range(rows // 8)], axis=0)
+            jnp.concatenate([in_ref[(2 * r + h) * 2 + c] for r in range(rows // 8)], axis=0)
             for c in range(2)
             for h in range(2)
         ],
         axis=1,
     )
     solved = lax.dot_general(
-        inverse,
+        inverse_ref[...],
         genes,
         (((1,), (0,)), ((), ())),
         precision=lax.Precision.HIGHEST,
@@ -197,14 +185,21 @@
 def on_device(expression, sketch_map):
     rows, genes = sketch_map.shape
     parts = lax.axis_size("z")
+    swap = [(0, 1), (1, 0)]
     mine, theirs = front(sketch_map, expression, parts)
-    summed = mine + lax.ppermute(theirs, "c", [(0, 1), (1, 0)])
-    arrived = lax.all_to_all(summed, ("y", "x"), 0, 0, tiled=True)
-    piece = small(spread_kernel, (parts, 16, 128), "spread", arrived)
-    arrived = lax.all_to_all(piece, "z", 0, 0, tiled=True)
-    piece = small(repeat_kernel, (lax.axis_size(WIDE), 16, 128), "repeat", arrived)
-    arrived = lax.all_to_all(piece, WIDE, 0, 0, tiled=True)
-    return small(tail_kernel, (rows, genes // parts), "tail", arrived)
+    summed = mine + lax.ppermute(theirs, "c", swap)
+    total = lax.all_to_all(summed, ("y", "x"), 0, 0, tiled=True).sum(axis=0)
+    ours = total[: 8 * parts].reshape(parts, 8, 128)
+    square = jnp.broadcast_to(total[None, 8 * parts :], (parts, rows // 4, 128))
+    piece = jnp.concatenate([ours, square], axis=1)
+    piece = lax.all_to_all(piece, "z", 0, 0, tiled=True).sum(axis=0)
+    spread = jnp.broadcast_to(piece[None, :8], (lax.axis_size(WIDE), 8, 128))
+    gathered = lax.all_to_all(spread, WIDE, 0, 0, tiled=True)
+    square = piece[8:]
+    inverse = small(
+        factor_kernel, (rows, rows), "factor", square, lax.ppermute(square, "c", swap)
+    )
+    return small(apply_kernel, (rows, genes // parts), "apply", inverse, gathered)
 
 
 def solution(mesh):

time: 70.2 us -> 64.5 us (0.919)
  blocking collectives: 48.3 us -> 32.8 us
  starting transfers between devices: 3.32 us -> 10.1 us
  waiting for transfers between devices: 1.63 us -> 4.57 us
  Pallas kernels: 16.5 us -> 14.5 us
  local copies, waits for them, and re-layouts: 0 us -> 1.93 us
    all_to_all x3 -> x2, blocking collectives: 48.3 us -> 32.8 us  [the longest x1 17.2 us: on_device(): total = lax.all_to_all(summed, ('y', 'x'), 0, 0, tiled=True).sum(axis=0)]
    all_to_all x0 -> x1, starting transfers between devices: none -> 6.39 us  [on_device(): gathered = lax.all_to_all(spread, WIDE, 0, 0, tiled=True)]
    pallas_call x3 -> x2, Pallas kernels: 7.7 us -> 5.67 us  [small(): pl.pallas_call(kernel, in_specs=[pl.BlockSpec(memory_space=pltpu.VMEM)] *...]
    all_to_all x0 -> x1, waiting for transfers between devices: none -> 2.02 us  [on_device(): gathered = lax.all_to_all(spread, WIDE, 0, 0, tiled=True)]
    unnamed x0 -> x6, local copies, waits for them, and re-layouts: none -> 1.24 us
    ppermute x1 -> x2, waiting for transfers between devices: 1.63 us -> 2.55 us  [the longest x1 1.72 us: on_device(): summed = mine + lax.ppermute(theirs, 'c', swap)]
    ppermute x1 -> x2, starting transfers between devices: 3.32 us -> 3.75 us  [the longest x1 3.32 us: on_device(): summed = mine + lax.ppermute(theirs, 'c', swap)]
  transfers between devices with their start and end apart: 1 -> 3, of which waited for: 1 -> 3; matrix products, arithmetic and copies ran while one was open for 0% -> 0% of each run, Pallas kernels for 0% -> 6%
where the time goes in v3:
time: 64.5 us; the launch traced here: 64.2 us
  blocking collectives  32.8 us (51%)
  Pallas kernels  14.5 us (22%)
  starting transfers between devices  10.1 us (16%)
  waiting for transfers between devices  4.57 us (7%)
  local copies, waits for them, and re-layouts  1.93 us (3%)
    all_to_all x1, blocking collectives, on_device(): total = lax.all_to_all(summed, ('y', 'x'), 0, 0, tiled=True).sum(axis=0)  17.2 us
    all_to_all x1, blocking collectives, on_device(): piece = lax.all_to_all(piece, 'z', 0, 0, tiled=True).sum(axis=0)  15.6 us
    pallas_call x1, Pallas kernels, front(): pl.pallas_call(functools.partial(front_kernel, parts, genes // parts), in...  8.82 us
    all_to_all x1, starting transfers between devices, on_device(): gathered = lax.all_to_all(spread, WIDE, 0, 0, tiled=True)  6.39 us
    pallas_call x2, Pallas kernels, small(): pl.pallas_call(kernel, in_specs=[pl.BlockSpec(memory_space=pltpu.VMEM)] *...  5.67 us
    ppermute x1, starting transfers between devices, on_device(): summed = mine + lax.ppermute(theirs, 'c', swap)  3.32 us
    all_to_all x1, waiting for transfers between devices, on_device(): gathered = lax.all_to_all(spread, WIDE, 0, 0, tiled=True)  2.02 us
    ppermute x1, waiting for transfers between devices, on_device(): summed = mine + lax.ppermute(theirs, 'c', swap)  1.72 us
  transfers between devices with their start and end apart: 3, of which 3 were waited for; matrix products, arithmetic and copies ran while one was open for 0% of the time, Pallas kernels for 6%

profile of v3, /device:TPU:1, one launch (start us, length us, event | category | flops | bytes accessed | tf_op | source)
XLA Modules:
  0.0 64.2 jit_solution(5399061774552691896)
XLA Ops:
  0.0 8.8 %front.1 = (f32[16,80,128]{2,1,0:T(8,128)S(1)}, f32[16,80,128]{2,1,0:T(8,128)S(1)}) custom-call(bf16[64,4000]{1,0:T(8,128)(2,1)} %s_hbm.1, bf16[4000,1536]{1,0:T(8,128)(2,1)} %e_hbm.1), custom_call_target="tpu_custom_call" | custom-call | tf_op jit(solution)/shard_map/front/pallas_call | solution.py:73
  8.8 3.3 %collective-permute-start = (f32[16,80,128]{2,1,0:T(8,128)S(1)}, f32[16,80,128]{2,1,0:T(8,128)S(1)}, u32[]{:S(2)}, u32[]{:S(2)}) collective-permute-start(f32[16,80,128]{2,1,0:T(8,128)S(1)} %get-tuple-element.8), channel_id=1, source_target_pairs={{0,8},{8,0},{1,9},{9,1},{2,10},{10,2},{3,11},{11,3},{4,12},{12,4},... | collective-permute-start | bytes 1966088 | tf_op jit(solution)/shard_map/ppermute | solution.py:190
  12.2 1.7 %collective-permute-done = f32[16,80,128]{2,1,0:T(8,128)S(1)} collective-permute-done((f32[16,80,128]{2,1,0:T(8,128)S(1)}, f32[16,80,128]{2,1,0:T(8,128)S(1)}, u32[]{:S(2)}, u32[]{:S(2)}) %collective-permute-start) | collective-permute-done | bytes 655392 | tf_op jit(solution)/shard_map/ppermute | solution.py:190
  13.9 0.1 add.3
  13.9 17.2 %all_to_all.15 = f32[16,80,128]{2,1,0:T(8,128)S(1)} all-to-all(f32[16,80,128]{2,1,0:T(8,128)S(1)} %add.3), channel_id=1, replica_groups=mesh['y'=4,'x'=4,'c'=2,'z'=8] {'y','x'}, dimensions={0} | all-to-all | bytes 1310720 | tf_op jit(solution)/shard_map/all_to_all | solution.py:191
  31.3 15.6 %all_to_all.16 = f32[8,24,128]{2,1,0:T(8,128)S(1)} all-to-all(f32[8,24,128]{2,1,0:T(8,128)S(1)} %pad_maximum_fusion), channel_id=1, replica_groups=mesh['y'=4,'x'=4,'c'=2,'z'=8] {'z'}, dimensions={0} | all-to-all | bytes 196608 | tf_op jit(solution)/shard_map/all_to_all | solution.py:195
  46.9 0.7 %broadcast_in_dim.5 = f32[32,8,128]{2,1,0:T(8,128)} broadcast(f32[8,128]{1,0:T(8,128)S(1)} %slice.19), dimensions={1,2} | broadcast | bytes 135168 | tf_op jit(solution)/shard_map/broadcast_in_dim | solution.py:196
  47.6 6.4 %all-to-all-start.2 = ((f32[32,8,128]{2,1,0:T(8,128)}), f32[32,8,128]{2,1,0:T(8,128)S(1)}, u32[]{:S(2)}, u32[]{:S(2)}) async-start(f32[32,8,128]{2,1,0:T(8,128)} %broadcast_in_dim.5), calls=%async_computation.2 | async-start | bytes 262144 | tf_op jit(solution)/shard_map/all_to_all | solution.py:197
  54.0 0.0 copy-start.1
  54.0 0.4 collective-permute-start.1
  54.4 0.8 %collective-permute-done.1.other_ref = f32[16,128]{1,0:T(8,128)S(1)} collective-permute-done((f32[16,128]{1,0:T(8,128)S(1)}, f32[16,128]{1,0:T(8,128)S(1)}, u32[]{:S(2)}, u32[]{:S(2)}) %collective-permute-start.1) | collective-permute-done | bytes 8224 | tf_op jit(solution)/shard_map/ppermute | solution.py:200
  55.2 0.0 copy-done.1
  55.2 0.0 copy-start.2
  55.2 0.6 copy-done.2
  55.8 3.8 %factor.1.inverse_ref = f32[64,64]{1,0:T(8,128)} custom-call(f32[16,128]{1,0:T(8,128)} %copy-done.1, f32[16,128]{1,0:T(8,128)} %copy-done.2), custom_call_target="tpu_custom_call" | custom-call | tf_op jit(solution)/shard_map/factor/pallas_call | solution.py:94
  59.7 2.0 %all-to-all-done.2.in_ref = f32[32,8,128]{2,1,0:T(8,128)S(1)} async-done(((f32[32,8,128]{2,1,0:T(8,128)}), f32[32,8,128]{2,1,0:T(8,128)S(1)}, u32[]{:S(2)}, u32[]{:S(2)}) %all-to-all-start.2) | async-done | bytes 131104 | tf_op jit(solution)/shard_map/all_to_all | solution.py:197
  61.7 0.0 copy-start
  61.7 0.6 %copy-done = f32[32,8,128]{2,1,0:T(8,128)} copy-done((f32[32,8,128]{2,1,0:T(8,128)}, f32[32,8,128]{2,1,0:T(8,128)S(1)}, u32[]{:S(2)}) %copy-start) | copy-done | bytes 131096
  62.3 1.8 %apply.1 = f32[64,500]{1,0:T(8,128)} custom-call(f32[64,64]{1,0:T(8,128)} %factor.1.inverse_ref, f32[32,8,128]{2,1,0:T(8,128)} %copy-done), custom_call_target="tpu_custom_call" | custom-call | tf_op jit(solution)/shard_map/apply/pallas_call | solution.py:94
  (8 shorter events, 0.1 us)
Async XLA Ops:
  8.8 5.0 %collective-permute-start = (f32[16,80,128]{2,1,0:T(8,128)S(1)}, f32[16,80,128]{2,1,0:T(8,128)S(1)}, u32[]{:S(2)}, u32[]{:S(2)}) collective-permute-start(f32[16,80,128]{2,1,0:T(8,128)S(1)} %get-tuple-element.8), channel_id=1, source_target_pairs={{0,8},{8,0},{1,9},{9,1},{2,10},{10,2},{3,11},{11,3},{4,12},{12,4},... | collective-permute-start | bytes 1966088 | tf_op jit(solution)/shard_map/ppermute | solution.py:190
  47.6 14.1 %all-to-all-start.2 = ((f32[32,8,128]{2,1,0:T(8,128)}), f32[32,8,128]{2,1,0:T(8,128)S(1)}, u32[]{:S(2)}, u32[]{:S(2)}) async-start(f32[32,8,128]{2,1,0:T(8,128)} %broadcast_in_dim.5), calls=%async_computation.2 | async-start | bytes 262144 | tf_op jit(solution)/shard_map/all_to_all | solution.py:197
  54.0 1.3 %copy-start.1 = (f32[16,128]{1,0:T(8,128)}, f32[16,128]{1,0:T(8,128)S(1)}, u32[]{:S(2)}) copy-start(f32[16,128]{1,0:T(8,128)S(1)} %slice.18.mine_ref) | copy-start | bytes 24580
  54.0 1.3 %collective-permute-start.1 = (f32[16,128]{1,0:T(8,128)S(1)}, f32[16,128]{1,0:T(8,128)S(1)}, u32[]{:S(2)}, u32[]{:S(2)}) collective-permute-start(f32[16,128]{1,0:T(8,128)S(1)} %slice.18.mine_ref), channel_id=1, source_target_pairs={{0,8},{8,0},{1,9},{9,1},{2,10},{10,2},{3,11},{11,3},{4,12},{12,4},... | collective-permute-start | bytes 24584 | tf_op jit(solution)/shard_map/ppermute | solution.py:200
  55.2 0.6 copy-start.2
  61.7 0.6 %copy-start = (f32[32,8,128]{2,1,0:T(8,128)}, f32[32,8,128]{2,1,0:T(8,128)S(1)}, u32[]{:S(2)}) copy-start(f32[32,8,128]{2,1,0:T(8,128)S(1)} %all-to-all-done.2.in_ref) | copy-start | bytes 393220

commit v4 on v3

--- a/solution.py
+++ b/solution.py
@@ -10,7 +10,7 @@
 
 WIDE = ("y", "x", "c")
 CHUNKS = (512, 512, 512)
-SPAN = 256
+EARLY = (0, 1024, 2048, 3072)
 
 
 def nn(a, b):
@@ -21,66 +21,84 @@
     return lax.dot_general(a, b, (((1,), (1,)), ((), ())), preferred_element_type=jnp.float32)
 
 
-def front_kernel(parts, share, s_hbm, e_hbm, mine_ref, theirs_ref, s_ref, *scratch):
+def front_kernel(parts, share, s_hbm, e_hbm, out_ref, s_ref, *scratch):
     count = len(CHUNKS)
     blocks = scratch[:count]
-    acc, gram, sems = scratch[count:]
+    acc, sems = scratch[count:]
     rows, genes = s_ref.shape
-    copies = [pltpu.make_async_copy(s_hbm, s_ref, sems.at[count])]
-    start = 0
-    for i, size in enumerate(CHUNKS):
-        copies.append(
-            pltpu.make_async_copy(e_hbm.at[:, pl.ds(start, size)], blocks[i], sems.at[i])
+    first = [pltpu.make_async_copy(s_hbm, s_ref, sems.at[count])]
+    for i, low in enumerate(EARLY):
+        size = (EARLY + (genes,))[i + 1] - low
+        first.append(
+            pltpu.make_async_copy(
+                e_hbm.at[pl.ds(low, size), pl.ds(0, CHUNKS[0])],
+                blocks[0].at[pl.ds(low, size)],
+                sems.at[count + 1 + i],
+            )
+        )
+    start, later = CHUNKS[0], []
+    for i, size in enumerate(CHUNKS[1:]):
+        later.append(
+            pltpu.make_async_copy(e_hbm.at[:, pl.ds(start, size)], blocks[i + 1], sems.at[i])
         )
         start += size
-    for copy in copies:
+    for copy in first + later:
         copy.start()
     acc[:, genes:] = jnp.zeros((rows, acc.shape[1] - genes), jnp.float32)
-    copies[0].wait()
-    total = None
+    first[0].wait()
+    square = None
     for i in range(count):
-        copies[i + 1].wait()
-        block = blocks[i][...]
-        sketched = nn(s_ref[...], block).astype(jnp.bfloat16)
-        square = nt(sketched, sketched)
-        total = square if i == 0 else total + square
         if i == 0:
-            acc[:, :genes] = nt(sketched, block)
+            sketched = None
+            for j, low in enumerate(EARLY):
+                first[j + 1].wait()
+                high = (EARLY + (genes,))[j + 1]
+                term = nn(s_ref[:, low:high], blocks[0][low:high, :])
+                sketched = term if j == 0 else sketched + term
         else:
-            acc[:, :genes] += nt(sketched, block)
+            later[i - 1].wait()
+            sketched = nn(s_ref[...], blocks[i][...])
+        sketched = sketched.astype(jnp.bfloat16)
+        term = nt(sketched, sketched)
+        square = term if i == 0 else square + term
+        if i == 0:
+            acc[:, :genes] = nt(sketched, blocks[i][...])
+        else:
+            acc[:, :genes] += nt(sketched, blocks[i][...])
+    lane = lax.broadcasted_iota(jnp.int32, (8, 128), 1)
+    for z in range(parts):
+        base, shift = z * share // 128, z * share % 128
+        for r in range(rows // 8):
+            held = [
+                acc[8 * r : 8 * r + 8, 128 * (base + t) : 128 * (base + t) + 128]
+                for t in range(5 if shift else 4)
+            ]
+            if shift:
+                held = [pltpu.roll(h, 128 - shift, 1) for h in held]
+                held = [jnp.where(lane < 128 - shift, p, q) for p, q in zip(held, held[1:])]
+            for t in range(4):
+                out_ref[t // 2, 2 * r + t % 2, 8 * z : 8 * z + 8, :] = held[t]
     quarter = rows // 4
     for h in range(2):
-        top = total[2 * quarter * h : 2 * quarter * h + quarter]
-        low = total[2 * quarter * h + quarter : 2 * quarter * (h + 1)]
-        gram[quarter * h : quarter * (h + 1), :] = jnp.concatenate([top, low], axis=1)
-    me = lax.axis_index("c")
-    for ref, core in ((mine_ref, me), (theirs_ref, 1 - me)):
-        for z in range(parts):
-            base, shift = z * share // 128 * 128, z * share % 128
-            wide = acc[:, pl.ds(pl.multiple_of(base + SPAN * core, 128), SPAN + 128)]
-            part = wide[:, shift : shift + SPAN]
-            for m in range(rows // 4):
-                r, c = m // 2 * 8, m % 2 * 128
-                ref[m, 8 * z : 8 * z + 8, :] = part[r : r + 8, c : c + 128]
-        half = gram[pl.ds(pl.multiple_of(quarter * core, 8), quarter), :]
+        top = square[2 * quarter * h : 2 * quarter * h + quarter]
+        low = square[2 * quarter * h + quarter : 2 * quarter * (h + 1)]
+        half = jnp.concatenate([top, low], axis=1)
         for m in range(quarter):
-            ref[m, 8 * parts :, :] = half
+            out_ref[h, m, 8 * parts :, :] = half
 
 
 def front(sketch_map, expression, parts):
     rows, genes = sketch_map.shape
-    out = jax.ShapeDtypeStruct((rows // 4, 8 * parts + rows // 4, 128), jnp.float32)
     return pl.pallas_call(
         functools.partial(front_kernel, parts, genes // parts),
         in_specs=[pl.BlockSpec(memory_space=pltpu.HBM)] * 2,
-        out_specs=[pl.BlockSpec(memory_space=pltpu.VMEM)] * 2,
-        out_shape=[out, out],
+        out_specs=pl.BlockSpec(memory_space=pltpu.VMEM),
+        out_shape=pltpu.VMEM((2, rows // 4, 8 * parts + rows // 4, 128), jnp.float32),
         scratch_shapes=[pltpu.VMEM((rows, genes), jnp.bfloat16)]
         + [pltpu.VMEM((genes, size), jnp.bfloat16) for size in CHUNKS]
         + [
-            pltpu.VMEM((rows, pl.cdiv(genes, 128) * 128), jnp.float32),
-            pltpu.VMEM((rows // 2, 2 * rows), jnp.float32),
-            pltpu.SemaphoreType.DMA((len(CHUNKS) + 1,)),
+            pltpu.VMEM((rows, parts // 2 * 1024 + 128), jnp.float32),
+            pltpu.SemaphoreType.DMA((len(CHUNKS) + 1 + len(EARLY),)),
         ],
         compiler_params=pltpu.CompilerParams(vmem_limit_bytes=40 << 20),
         name="front",
@@ -90,12 +108,12 @@
     )
 
 
-def small(kernel, shape, name, *args):
+def small(kernel, shape, name, *args, space=jax.ShapeDtypeStruct):
     return pl.pallas_call(
         kernel,
         in_specs=[pl.BlockSpec(memory_space=pltpu.VMEM)] * len(args),
         out_specs=pl.BlockSpec(memory_space=pltpu.VMEM),
-        out_shape=jax.ShapeDtypeStruct(shape, jnp.float32),
+        out_shape=space(shape, jnp.float32),
         name=name,
     )(*args)
 
@@ -182,11 +200,18 @@
     out_ref[...] = solved[:, :share]
 
 
+def near(x):
+    return pltpu.with_memory_space_constraint(x, pltpu.VMEM)
+
+
 def on_device(expression, sketch_map):
     rows, genes = sketch_map.shape
     parts = lax.axis_size("z")
     swap = [(0, 1), (1, 0)]
-    mine, theirs = front(sketch_map, expression, parts)
+    me = lax.axis_index("c")
+    halves = front(sketch_map, expression, parts)
+    mine = lax.dynamic_index_in_dim(halves, me, 0, keepdims=False)
+    theirs = lax.dynamic_index_in_dim(halves, 1 - me, 0, keepdims=False)
     summed = mine + lax.ppermute(theirs, "c", swap)
     total = lax.all_to_all(summed, ("y", "x"), 0, 0, tiled=True).sum(axis=0)
     ours = total[: 8 * parts].reshape(parts, 8, 128)
@@ -194,12 +219,13 @@
     piece = jnp.concatenate([ours, square], axis=1)
     piece = lax.all_to_all(piece, "z", 0, 0, tiled=True).sum(axis=0)
     spread = jnp.broadcast_to(piece[None, :8], (lax.axis_size(WIDE), 8, 128))
-    gathered = lax.all_to_all(spread, WIDE, 0, 0, tiled=True)
+    gathered = near(lax.all_to_all(near(spread), WIDE, 0, 0, tiled=True))
     square = piece[8:]
+    other = near(lax.ppermute(square, "c", swap))
     inverse = small(
-        factor_kernel, (rows, rows), "factor", square, lax.ppermute(square, "c", swap)
-    )
-    return small(apply_kernel, (rows, genes // parts), "apply", inverse, gathered)
+        factor_kernel, (rows, rows), "factor", near(square), other, space=pltpu.VMEM
+    )
+    return small(apply_kernel, (rows, genes // parts), "apply", near(inverse), gathered)
 
 
 def solution(mesh):

time: 64.5 us -> 62.4 us (0.967)
  Pallas kernels: 14.5 us -> 11.7 us
  waiting for transfers between devices: 4.57 us -> 6.51 us
  local copies, waits for them, and re-layouts: 1.93 us -> 0.74 us
    pallas_call x2, Pallas kernels: 5.67 us -> 3.41 us  [small(): pl.pallas_call(kernel, in_specs=[pl.BlockSpec(memory_space=pltpu.VMEM)] *...]
    all_to_all x1, waiting for transfers between devices: 2.02 us -> 3.96 us  [on_device(): gathered = near(lax.all_to_all(near(spread), WIDE, 0, 0, tiled=True))]
    unnamed x6 -> x0, local copies, waits for them, and re-layouts: 1.24 us -> none
  transfers between devices with their start and end apart: 3 -> 3, of which waited for: 3 -> 3; matrix products, arithmetic and copies ran while one was open for 0% -> 0% of each run, Pallas kernels for 6% -> 4%
where the time goes in v4:
time: 62.4 us; the launch traced here: 62.2 us
  blocking collectives  32.8 us (53%)
  Pallas kernels  11.7 us (19%)
  starting transfers between devices  10.2 us (16%)
  waiting for transfers between devices  6.51 us (10%)
  local copies, waits for them, and re-layouts  0.74 us (1%)
    all_to_all x1, blocking collectives, on_device(): total = lax.all_to_all(summed, ('y', 'x'), 0, 0, tiled=True).sum(axis=0)  17.2 us
    all_to_all x1, blocking collectives, on_device(): piece = lax.all_to_all(piece, 'z', 0, 0, tiled=True).sum(axis=0)  15.6 us
    pallas_call x1, Pallas kernels, front(): pl.pallas_call(functools.partial(front_kernel, parts, genes // parts), in...  8.34 us
    all_to_all x1, starting transfers between devices, on_device(): gathered = near(lax.all_to_all(near(spread), WIDE, 0, 0, tiled=True))  6.39 us
    all_to_all x1, waiting for transfers between devices, on_device(): gathered = near(lax.all_to_all(near(spread), WIDE, 0, 0, tiled=True))  3.96 us
    pallas_call x2, Pallas kernels, small(): pl.pallas_call(kernel, in_specs=[pl.BlockSpec(memory_space=pltpu.VMEM)] *...  3.41 us
    ppermute x1, starting transfers between devices, on_device(): summed = mine + lax.ppermute(theirs, 'c', swap)  3.33 us
    ppermute x1, waiting for transfers between devices, on_device(): summed = mine + lax.ppermute(theirs, 'c', swap)  1.72 us
  transfers between devices with their start and end apart: 3, of which 3 were waited for; matrix products, arithmetic and copies ran while one was open for 0% of the time, Pallas kernels for 4%

profile of v4, /device:TPU:1, one launch (start us, length us, event | category | flops | bytes accessed | tf_op | source)
XLA Modules:
  0.0 62.2 jit_solution(3118560971765060859)
XLA Ops:
  0.0 8.3 %front.1 = f32[2,16,80,128]{3,2,1,0:T(8,128)S(1)} custom-call(bf16[64,4000]{1,0:T(8,128)(2,1)} %s_hbm.1, bf16[4000,1536]{1,0:T(8,128)(2,1)} %e_hbm.1), custom_call_target="tpu_custom_call" | custom-call | tf_op jit(solution)/shard_map/front/pallas_call | solution.py:92
  8.3 0.1 dynamic-slice_bitcast_fusion
  8.4 3.3 %collective-permute-start = (f32[16,80,128]{2,1,0:T(8,128)S(1)}, f32[16,80,128]{2,1,0:T(8,128)S(1)}, u32[]{:S(2)}, u32[]{:S(2)}) collective-permute-start(f32[16,80,128]{2,1,0:T(8,128)S(1)} %dynamic-slice_bitcast_fusion), channel_id=1, source_target_pairs={{0,8},{8,0},{1,9},{9,1},{2,10},{10,2},{3,11},{11,3},{4,12},{12,4},... | collective-permute-start | bytes 1966088 | tf_op jit(solution)/shard_map/ppermute | solution.py:215
  11.7 1.7 %collective-permute-done = f32[16,80,128]{2,1,0:T(8,128)S(1)} collective-permute-done((f32[16,80,128]{2,1,0:T(8,128)S(1)}, f32[16,80,128]{2,1,0:T(8,128)S(1)}, u32[]{:S(2)}, u32[]{:S(2)}) %collective-permute-start) | collective-permute-done | bytes 655392 | tf_op jit(solution)/shard_map/ppermute | solution.py:215
  13.5 0.1 bitcast_add_fusion
  13.5 17.2 %all_to_all.15 = f32[16,80,128]{2,1,0:T(8,128)S(1)} all-to-all(f32[16,80,128]{2,1,0:T(8,128)S(1)} %bitcast_add_fusion), channel_id=1, replica_groups=mesh['y'=4,'x'=4,'c'=2,'z'=8] {'y','x'}, dimensions={0} | all-to-all | bytes 1310720 | tf_op jit(solution)/shard_map/all_to_all | solution.py:216
  30.9 15.6 %all_to_all.16 = f32[8,24,128]{2,1,0:T(8,128)S(1)} all-to-all(f32[8,24,128]{2,1,0:T(8,128)S(1)} %pad_maximum_fusion), channel_id=1, replica_groups=mesh['y'=4,'x'=4,'c'=2,'z'=8] {'z'}, dimensions={0} | all-to-all | bytes 196608 | tf_op jit(solution)/shard_map/all_to_all | solution.py:220
  46.5 0.7 %broadcast_in_dim.5 = f32[32,8,128]{2,1,0:T(8,128)} broadcast(f32[8,128]{1,0:T(8,128)S(1)} %slice.19), dimensions={1,2} | broadcast | bytes 135168 | tf_op jit(solution)/shard_map/broadcast_in_dim | solution.py:221
  47.1 6.4 %all-to-all-start.2 = ((f32[32,8,128]{2,1,0:T(8,128)}), f32[32,8,128]{2,1,0:T(8,128)S(1)}, u32[]{:S(2)}, u32[]{:S(2)}) async-start(f32[32,8,128]{2,1,0:T(8,128)} %broadcast_in_dim.5), calls=%async_computation.2 | async-start | bytes 262144 | tf_op jit(solution)/shard_map/all_to_all | solution.py:222
  53.6 0.4 collective-permute-start.1
  54.0 0.8 %collective-permute-done.1.other_ref = f32[16,128]{1,0:T(8,128)S(1)} collective-permute-done((f32[16,128]{1,0:T(8,128)S(1)}, f32[16,128]{1,0:T(8,128)S(1)}, u32[]{:S(2)}, u32[]{:S(2)}) %collective-permute-start.1) | collective-permute-done | bytes 8224 | tf_op jit(solution)/shard_map/ppermute | solution.py:224
  54.8 2.5 %factor.1.inverse_ref = f32[64,64]{1,0:T(8,128)S(1)} custom-call(f32[16,128]{1,0:T(8,128)S(1)} %slice.18.mine_ref, f32[16,128]{1,0:T(8,128)S(1)} %collective-permute-done.1.other_ref), custom_call_target="tpu_custom_call" | custom-call | tf_op jit(solution)/shard_map/factor/pallas_call | solution.py:112
  57.3 4.0 %all-to-all-done.2.in_ref = f32[32,8,128]{2,1,0:T(8,128)S(1)} async-done(((f32[32,8,128]{2,1,0:T(8,128)}), f32[32,8,128]{2,1,0:T(8,128)S(1)}, u32[]{:S(2)}, u32[]{:S(2)}) %all-to-all-start.2) | async-done | bytes 131104 | tf_op jit(solution)/shard_map/all_to_all | solution.py:222
  61.3 0.9 %apply.1 = f32[64,500]{1,0:T(8,128)} custom-call(f32[64,64]{1,0:T(8,128)S(1)} %factor.1.inverse_ref, f32[32,8,128]{2,1,0:T(8,128)S(1)} %all-to-all-done.2.in_ref), custom_call_target="tpu_custom_call" | custom-call | tf_op jit(solution)/shard_map/apply/pallas_call | solution.py:112
  (8 shorter events, 0.1 us)
Async XLA Ops:
  8.4 5.1 %collective-permute-start = (f32[16,80,128]{2,1,0:T(8,128)S(1)}, f32[16,80,128]{2,1,0:T(8,128)S(1)}, u32[]{:S(2)}, u32[]{:S(2)}) collective-permute-start(f32[16,80,128]{2,1,0:T(8,128)S(1)} %dynamic-slice_bitcast_fusion), channel_id=1, source_target_pairs={{0,8},{8,0},{1,9},{9,1},{2,10},{10,2},{3,11},{11,3},{4,12},{12,4},... | collective-permute-start | bytes 1966088 | tf_op jit(solution)/shard_map/ppermute | solution.py:215
  47.1 14.1 %all-to-all-start.2 = ((f32[32,8,128]{2,1,0:T(8,128)}), f32[32,8,128]{2,1,0:T(8,128)S(1)}, u32[]{:S(2)}, u32[]{:S(2)}) async-start(f32[32,8,128]{2,1,0:T(8,128)} %broadcast_in_dim.5), calls=%async_computation.2 | async-start | bytes 262144 | tf_op jit(solution)/shard_map/all_to_all | solution.py:222
  53.6 1.3 %collective-permute-start.1 = (f32[16,128]{1,0:T(8,128)S(1)}, f32[16,128]{1,0:T(8,128)S(1)}, u32[]{:S(2)}, u32[]{:S(2)}) collective-permute-start(f32[16,128]{1,0:T(8,128)S(1)} %slice.18.mine_ref), channel_id=1, source_target_pairs={{0,8},{8,0},{1,9},{9,1},{2,10},{10,2},{3,11},{11,3},{4,12},{12,4},... | collective-permute-start | bytes 24584 | tf_op jit(solution)/shard_map/ppermute | solution.py:224

commit v5 on v3

v5 whole, which is shorter than its diff:
```python
import functools

import jax
import jax.numpy as jnp
from jax import lax
from jax.experimental import pallas as pl
from jax.experimental.pallas import tpu as pltpu
from jax.sharding import Mesh
from jax.sharding import PartitionSpec as P

WIDE = ("y", "x", "c")
PIECES = (1024, 1024, 1024, 928)
BLOCKS = (512, 512, 512)
SPAN = 256


def nn(a, b):
    return lax.dot_general(a, b, (((1,), (0,)), ((), ())), preferred_element_type=jnp.float32)


def nt(a, b):
    return lax.dot_general(a, b, (((1,), (1,)), ((), ())), preferred_element_type=jnp.float32)


def window_start(z, share):
    return z * share // 16 * 16


def put_products(ref, core, parts, share, sketched, e_ref, cells=slice(None), add=False):
    for z in range(parts):
        start = pl.multiple_of(window_start(z, share) + SPAN * core, 16)
        part = nt(sketched, e_ref[pl.ds(start, SPAN), cells])
        for m in range(ref.shape[0]):
            r, c = m // 2 * 8, m % 2 * 128
            tile = part[r : r + 8, c : c + 128]
            if add:
                tile = ref[m, 8 * z : 8 * z + 8, :] + tile
            ref[m, 8 * z : 8 * z + 8, :] = tile


def put_gram(ref, core, parts, gram_ref):
    half = gram_ref[core]
    for m in range(ref.shape[0]):
        ref[m, 8 * parts :, :] = half


def begin_kernel(parts, share, s_hbm, e_hbm, theirs_ref, sketched_ref, gram_ref, e_ref, *scratch):
    s_ref, acc, sems = scratch
    count = len(PIECES)
    spans = [slice(sum(PIECES[:i]), sum(PIECES[: i + 1])) for i in range(count)]
    blocks = [slice(sum(BLOCKS[:j]), sum(BLOCKS[: j + 1])) for j in range(len(BLOCKS))]
    whole = pltpu.make_async_copy(s_hbm, s_ref, sems.at[count * len(BLOCKS)])
    whole.start()
    copies = []
    for j, block in enumerate(blocks):
        for i, span in enumerate(spans):
            where = (pl.ds(span.start, PIECES[i]), pl.ds(block.start, BLOCKS[j]))
            copy = pltpu.make_async_copy(e_hbm.at[where], e_ref.at[where], sems.at[j * count + i])
            copy.start()
            copies.append(copy)
    whole.wait()
    core = 1 - lax.axis_index("c")
    square = None
    for j, block in enumerate(blocks):
        for i, span in enumerate(spans):
            copies[j * count + i].wait()
            term = nn(s_ref[:, span], e_ref[span, block])
            if i > 0:
                term = acc[:, : BLOCKS[j]] + term
            if i < count - 1:
                acc[:, : BLOCKS[j]] = term
        sketched = term.astype(jnp.bfloat16)
        sketched_ref[:, block] = sketched
        term = nt(sketched, sketched)
        square = term if j == 0 else square + term
        put_products(theirs_ref, core, parts, share, sketched, e_ref, block, j > 0)
    quarter = square.shape[0] // 4
    for h in range(2):
        top = square[2 * quarter * h : 2 * quarter * h + quarter]
        low = square[2 * quarter * h + quarter : 2 * quarter * (h + 1)]
        gram_ref[h] = jnp.concatenate([top, low], axis=1)
    put_gram(theirs_ref, core, parts, gram_ref)


def finish_kernel(parts, share, sketched_ref, gram_ref, e_ref, mine_ref):
    core = lax.axis_index("c")
    put_gram(mine_ref, core, parts, gram_ref)
    put_products(mine_ref, core, parts, share, sketched_ref[...], e_ref)


def begin(sketch_map, expression, parts):
    rows, genes = sketch_map.shape
    cells = expression.shape[1]
    return pl.pallas_call(
        functools.partial(begin_kernel, parts, genes // parts),
        in_specs=[pl.BlockSpec(memory_space=pltpu.HBM)] * 2,
        out_specs=[pl.BlockSpec(memory_space=pltpu.VMEM)] * 4,
        out_shape=[
            pltpu.VMEM((rows // 4, 8 * parts + rows // 4, 128), jnp.float32),
            pltpu.VMEM((rows, cells), jnp.bfloat16),
            pltpu.VMEM((2, rows // 4, 128), jnp.float32),
            pltpu.VMEM((genes, cells), jnp.bfloat16),
        ],
        scratch_shapes=[
            pltpu.VMEM((rows, genes), jnp.bfloat16),
            pltpu.VMEM((rows, max(BLOCKS)), jnp.float32),
            pltpu.SemaphoreType.DMA((len(PIECES) * len(BLOCKS) + 1,)),
        ],
        compiler_params=pltpu.CompilerParams(vmem_limit_bytes=24 << 20),
        name="begin",
    )(
        pltpu.with_memory_space_constraint(sketch_map, pltpu.HBM),
        pltpu.with_memory_space_constraint(expression, pltpu.HBM),
    )


def finish(sketched, gram, expression, parts):
    genes, cells = expression.shape
    rows = sketched.shape[0]
    return pl.pallas_call(
        functools.partial(finish_kernel, parts, genes // parts),
        in_specs=[pl.BlockSpec(memory_space=pltpu.VMEM)] * 3,
        out_specs=pl.BlockSpec(memory_space=pltpu.VMEM),
        out_shape=pltpu.VMEM((rows // 4, 8 * parts + rows // 4, 128), jnp.float32),
        cost_estimate=pl.CostEstimate(
            flops=rows * genes * cells, bytes_accessed=genes * cells * 2, transcendentals=0
        ),
        compiler_params=pltpu.CompilerParams(vmem_limit_bytes=24 << 20),
        name="finish",
    )(near(sketched), near(gram), near(expression))


def small(kernel, shape, name, *args, space=jax.ShapeDtypeStruct):
    return pl.pallas_call(
        kernel,
        in_specs=[pl.BlockSpec(memory_space=pltpu.VMEM)] * len(args),
        out_specs=pl.BlockSpec(memory_space=pltpu.VMEM),
        out_shape=space(shape, jnp.float32),
        name=name,
    )(*args)


def over_tile(x):
    return jnp.broadcast_to(x, (8, 128))


def inverse_factor(work, sub):
    count = len(work)
    for g in range(count):
        block = work[g]
        at = 64 + 8 * g
        columns = [over_tile(block[:, at + j : at + j + 1]) for j in range(8)]
        a = {(i, j): over_tile(columns[j][i : i + 1]) for j in range(8) for i in range(j, 8)}
        rows = [over_tile(block[i : i + 1]) for i in range(8)]
        low, inverse = {}, []
        for j in range(8):
            inverse.append(1.0 / a[j, j])
            for i in range(j + 1, 8):
                low[i, j] = a[i, j] * inverse[j]
            for i in range(j + 1, 8):
                for m in range(j + 1, i + 1):
                    a[i, m] = a[i, m] - low[i, j] * a[m, j]
        solved = []
        for i in range(8):
            row = rows[i]
            for j in range(i):
                row = row - low[i, j] * solved[j]
            solved.append(row)
        if g < count - 1:
            back = [None] * 8
            for i in reversed(range(8)):
                row = solved[i] * inverse[i]
                for j in range(i + 1, 8):
                    row = row - low[j, i] * back[j]
                back[i] = row
            for h in range(g + 1, count):
                left = work[h]
                for j in range(8):
                    left = left - over_tile(work[h][:, at + j : at + j + 1]) * back[j]
                work[h] = left
        block, pivots = solved[0], a[0, 0]
        for i in range(1, 8):
            block = jnp.where(sub == i, solved[i], block)
            pivots = jnp.where(sub == i, a[i, i], pivots)
        work[g] = block * lax.rsqrt(pivots)
    return work


def factor_kernel(mine_ref, other_ref, out_ref):
    me = lax.axis_index("c")
    mine, other = mine_ref[...], other_ref[...]
    halves = [jnp.where(me == 0, mine, other), jnp.where(me == 0, other, mine)]
    sub = lax.broadcasted_iota(jnp.int32, (8, 128), 0)
    lane = lax.broadcasted_iota(jnp.int32, (8, 128), 1)
    work = []
    for g in range(8):
        held = halves[g // 4][8 * (g % 2) : 8 * (g % 2) + 8]
        if g // 2 % 2 == 0:
            held = pltpu.roll(held, 64, 1)
        work.append(jnp.where(lane < 64, jnp.where(lane == sub + 8 * g, 1.0, 0.0), held))
    for g, block in enumerate(inverse_factor(work, sub)):
        out_ref[8 * g : 8 * g + 8, :] = block[:, :64]


def apply_kernel(parts, inverse_ref, in_ref, out_ref):
    rows, share = out_ref.shape
    genes = jnp.concatenate(
        [
            jnp.concatenate([in_ref[(2 * r + h) * 2 + c] for r in range(rows // 8)], axis=0)
            for c in range(2)
            for h in range(2)
        ],
        axis=1,
    )
    solved = lax.dot_general(
        inverse_ref[...],
        genes,
        (((1,), (0,)), ((), ())),
        precision=lax.Precision.HIGHEST,
        preferred_element_type=jnp.float32,
    )
    extra = lax.axis_index("z") * share % 16
    for shift in sorted({z * share % 16 for z in range(parts)}):

        @pl.when(extra == shift)
        def _():
            out_ref[...] = solved[:, shift : shift + share]


def near(x):
    return pltpu.with_memory_space_constraint(x, pltpu.VMEM)


def on_device(expression, sketch_map):
    rows, genes = sketch_map.shape
    parts = lax.axis_size("z")
    swap = [(0, 1), (1, 0)]
    theirs, sketched, gram, held = begin(sketch_map, expression, parts)
    theirs = lax.ppermute(theirs, "c", swap)
    summed = finish(sketched, gram, held, parts) + theirs
    total = lax.all_to_all(summed, ("y", "x"), 0, 0, tiled=True).sum(axis=0)
    ours = total[: 8 * parts].reshape(parts, 8, 128)
    square = jnp.broadcast_to(total[None, 8 * parts :], (parts, rows // 4, 128))
    piece = jnp.concatenate([ours, square], axis=1)
    piece = lax.all_to_all(piece, "z", 0, 0, tiled=True).sum(axis=0)
    spread = jnp.broadcast_to(piece[None, :8], (lax.axis_size(WIDE), 8, 128))
    gathered = near(lax.all_to_all(near(spread), WIDE, 0, 0, tiled=True))
    square = piece[8:]
    other = near(lax.ppermute(square, "c", swap))
    inverse = small(
        factor_kernel, (rows, rows), "factor", near(square), other, space=pltpu.VMEM
    )
    return small(
        functools.partial(apply_kernel, parts),
        (rows, genes // parts),
        "apply",
        near(inverse),
        gathered,
    )


def solution(mesh):
    grid = Mesh(mesh.devices.reshape(4, 4, 2, 8), ("y", "x", "c", "z"))
    placed = (P(None, ("y", "x", "c", "z")), P())
    return jax.shard_map(
        on_device, mesh=grid, in_specs=placed, out_specs=P(None, "z"), check_vma=False
    )
```

time: 64.5 us -> 60.8 us (0.943)
  Pallas kernels: 14.5 us -> 11.8 us
  local copies, waits for them, and re-layouts: 1.93 us -> 0.68 us
    pallas_call x2, Pallas kernels: 5.67 us -> 3.43 us  [small(): pl.pallas_call(kernel, in_specs=[pl.BlockSpec(memory_space=pltpu.VMEM)] *...]
    all_to_all x1, waiting for transfers between devices: 2.02 us -> 3.96 us  [on_device(): gathered = near(lax.all_to_all(near(spread), WIDE, 0, 0, tiled=True))]
    ppermute x2, waiting for transfers between devices: 2.55 us -> 0.83 us  [the longest x1 0.83 us: on_device(): other = near(lax.ppermute(square, 'c', swap))]
    unnamed x6 -> x0, local copies, waits for them, and re-layouts: 1.24 us -> none
    pallas_call x1 -> x2, Pallas kernels: 8.82 us -> 8.4 us  [the longest x1 6.4 us: begin(): pl.pallas_call(functools.partial(begin_kernel, parts, genes // parts), in...]
  transfers between devices with their start and end apart: 3 -> 3, of which waited for: 3 -> 2; matrix products, arithmetic and copies ran while one was open for 0% -> 0% of each run, Pallas kernels for 6% -> 7%
where the time goes in v5:
time: 60.8 us; the launch traced here: 60.5 us
  blocking collectives  33.1 us (54%)
  Pallas kernels  11.8 us (19%)
  starting transfers between devices  9.89 us (16%)
  waiting for transfers between devices  4.79 us (8%)
  local copies, waits for them, and re-layouts  0.68 us (1%)
    all_to_all x1, blocking collectives, on_device(): total = lax.all_to_all(summed, ('y', 'x'), 0, 0, tiled=True).sum(axis=0)  17.5 us
    all_to_all x1, blocking collectives, on_device(): piece = lax.all_to_all(piece, 'z', 0, 0, tiled=True).sum(axis=0)  15.6 us
    pallas_call x1, Pallas kernels, begin(): pl.pallas_call(functools.partial(begin_kernel, parts, genes // parts), in...  6.4 us
    all_to_all x1, starting transfers between devices, on_device(): gathered = near(lax.all_to_all(near(spread), WIDE, 0, 0, tiled=True))  6.12 us
    all_to_all x1, waiting for transfers between devices, on_device(): gathered = near(lax.all_to_all(near(spread), WIDE, 0, 0, tiled=True))  3.96 us
    pallas_call x2, Pallas kernels, small(): pl.pallas_call(kernel, in_specs=[pl.BlockSpec(memory_space=pltpu.VMEM)] *...  3.43 us
    ppermute x1, starting transfers between devices, on_device(): theirs = lax.ppermute(theirs, 'c', swap)  3.33 us
    pallas_call x1, Pallas kernels, finish(): pl.pallas_call(functools.partial(finish_kernel, parts, genes // parts), i...  1.99 us
  transfers between devices with their start and end apart: 3, of which 2 were waited for; matrix products, arithmetic and copies ran while one was open for 0% of the time, Pallas kernels for 7%

profile of v5, /device:TPU:1, one launch (start us, length us, event | category | flops | bytes accessed | tf_op | source)
XLA Modules:
  0.0 60.5 jit_solution(4475221013036485978)
XLA Ops:
  0.0 6.4 %begin.1 = (f32[16,80,128]{2,1,0:T(8,128)S(1)}, bf16[64,1536]{1,0:T(8,128)(2,1)S(1)}, f32[2,16,128]{2,1,0:T(8,128)S(1)}, bf16[4000,1536]{1,0:T(8,128)(2,1)S(1)}) custom-call(bf16[64,4000]{1,0:T(8,128)(2,1)} %s_hbm.1, bf16[4000,1536]{1,0:T(8,128)(2,1)} %e_hbm.1), custom_call_target="tpu_custom_call" | custom-call | tf_op jit(solution)/shard_map/begin/pallas_call | solution.py:94
  6.4 3.3 %collective-permute-start = (f32[16,80,128]{2,1,0:T(8,128)S(1)}, f32[16,80,128]{2,1,0:T(8,128)S(1)}, u32[]{:S(2)}, u32[]{:S(2)}) collective-permute-start(f32[16,80,128]{2,1,0:T(8,128)S(1)} %get-tuple-element.12), channel_id=1, source_target_pairs={{0,8},{8,0},{1,9},{9,1},{2,10},{10,2},{3,11},{11,3},{4,12},{12,4},... | collective-permute-start | bytes 1966088 | tf_op jit(solution)/shard_map/ppermute | solution.py:239
  9.7 2.0 %finish.1 = f32[16,80,128]{2,1,0:T(8,128)S(1)} custom-call(bf16[64,1536]{1,0:T(8,128)(2,1)S(1)} %get-tuple-element.9.sketched_ref, f32[2,16,128]{2,1,0:T(8,128)S(1)} %get-tuple-element.10.gram_ref, bf16[4000,1536]{1,0:T(8,128)(2,1)S(1)} %get-tuple-element.11.e_ref), custom_call_target="tpu_custom_call" | custom-call | flops 393216000 | bytes 12288000 | tf_op jit(solution)/shard_map/finish/pallas_call | solution.py:120
  11.7 0.0 collective-permute-done
  11.8 0.1 add.3
  11.8 17.5 %all_to_all.15 = f32[16,80,128]{2,1,0:T(8,128)S(1)} all-to-all(f32[16,80,128]{2,1,0:T(8,128)S(1)} %add.3), channel_id=1, replica_groups=mesh['y'=4,'x'=4,'c'=2,'z'=8] {'y','x'}, dimensions={0} | all-to-all | bytes 1310720 | tf_op jit(solution)/shard_map/all_to_all | solution.py:241
  29.5 15.6 %all_to_all.16 = f32[8,24,128]{2,1,0:T(8,128)S(1)} all-to-all(f32[8,24,128]{2,1,0:T(8,128)S(1)} %pad_maximum_fusion), channel_id=1, replica_groups=mesh['y'=4,'x'=4,'c'=2,'z'=8] {'z'}, dimensions={0} | all-to-all | bytes 196608 | tf_op jit(solution)/shard_map/all_to_all | solution.py:245
  45.1 0.7 %broadcast_in_dim.5 = f32[32,8,128]{2,1,0:T(8,128)} broadcast(f32[8,128]{1,0:T(8,128)S(1)} %slice.19), dimensions={1,2} | broadcast | bytes 135168 | tf_op jit(solution)/shard_map/broadcast_in_dim | solution.py:246
  45.7 6.1 %all-to-all-start.2 = ((f32[32,8,128]{2,1,0:T(8,128)}), f32[32,8,128]{2,1,0:T(8,128)S(1)}, u32[]{:S(2)}, u32[]{:S(2)}) async-start(f32[32,8,128]{2,1,0:T(8,128)} %broadcast_in_dim.5), calls=%async_computation.2 | async-start | bytes 262144 | tf_op jit(solution)/shard_map/all_to_all | solution.py:247
  51.9 0.4 collective-permute-start.1
  52.3 0.8 %collective-permute-done.1.other_ref = f32[16,128]{1,0:T(8,128)S(1)} collective-permute-done((f32[16,128]{1,0:T(8,128)S(1)}, f32[16,128]{1,0:T(8,128)S(1)}, u32[]{:S(2)}, u32[]{:S(2)}) %collective-permute-start.1) | collective-permute-done | bytes 8224 | tf_op jit(solution)/shard_map/ppermute | solution.py:249
  53.1 2.5 %factor.1.inverse_ref = f32[64,64]{1,0:T(8,128)S(1)} custom-call(f32[16,128]{1,0:T(8,128)S(1)} %slice.18.mine_ref, f32[16,128]{1,0:T(8,128)S(1)} %collective-permute-done.1.other_ref), custom_call_target="tpu_custom_call" | custom-call | tf_op jit(solution)/shard_map/factor/pallas_call | solution.py:134
  55.7 4.0 %all-to-all-done.2.in_ref = f32[32,8,128]{2,1,0:T(8,128)S(1)} async-done(((f32[32,8,128]{2,1,0:T(8,128)}), f32[32,8,128]{2,1,0:T(8,128)S(1)}, u32[]{:S(2)}, u32[]{:S(2)}) %all-to-all-start.2) | async-done | bytes 131104 | tf_op jit(solution)/shard_map/all_to_all | solution.py:247
  59.6 0.9 %apply.1 = f32[64,500]{1,0:T(8,128)} custom-call(f32[64,64]{1,0:T(8,128)S(1)} %factor.1.inverse_ref, f32[32,8,128]{2,1,0:T(8,128)S(1)} %all-to-all-done.2.in_ref), custom_call_target="tpu_custom_call" | custom-call | tf_op jit(solution)/shard_map/apply/pallas_call | solution.py:134
  (8 shorter events, 0.1 us)
Async XLA Ops:
  6.4 5.3 %collective-permute-start = (f32[16,80,128]{2,1,0:T(8,128)S(1)}, f32[16,80,128]{2,1,0:T(8,128)S(1)}, u32[]{:S(2)}, u32[]{:S(2)}) collective-permute-start(f32[16,80,128]{2,1,0:T(8,128)S(1)} %get-tuple-element.12), channel_id=1, source_target_pairs={{0,8},{8,0},{1,9},{9,1},{2,10},{10,2},{3,11},{11,3},{4,12},{12,4},... | collective-permute-start | bytes 1966088 | tf_op jit(solution)/shard_map/ppermute | solution.py:239
  45.7 13.9 %all-to-all-start.2 = ((f32[32,8,128]{2,1,0:T(8,128)}), f32[32,8,128]{2,1,0:T(8,128)S(1)}, u32[]{:S(2)}, u32[]{:S(2)}) async-start(f32[32,8,128]{2,1,0:T(8,128)} %broadcast_in_dim.5), calls=%async_computation.2 | async-start | bytes 262144 | tf_op jit(solution)/shard_map/all_to_all | solution.py:247
  51.9 1.3 %collective-permute-start.1 = (f32[16,128]{1,0:T(8,128)S(1)}, f32[16,128]{1,0:T(8,128)S(1)}, u32[]{:S(2)}, u32[]{:S(2)}) collective-permute-start(f32[16,128]{1,0:T(8,128)S(1)} %slice.18.mine_ref), channel_id=1, source_target_pairs={{0,8},{8,0},{1,9},{9,1},{2,10},{10,2},{3,11},{11,3},{4,12},{12,4},... | collective-permute-start | bytes 24584 | tf_op jit(solution)/shard_map/ppermute | solution.py:249

commit v6 on v5

--- a/solution.py
+++ b/solution.py
@@ -5,10 +5,8 @@
 from jax import lax
 from jax.experimental import pallas as pl
 from jax.experimental.pallas import tpu as pltpu
-from jax.sharding import Mesh
 from jax.sharding import PartitionSpec as P
 
-WIDE = ("y", "x", "c")
 PIECES = (1024, 1024, 1024, 928)
 BLOCKS = (512, 512, 512)
 SPAN = 256
@@ -26,22 +24,29 @@
     return z * share // 16 * 16
 
 
+def place():
+    index = lax.axis_index("wide")
+    core, x, y = index & 1, (index >> 1) & 3, index >> 3
+    along_x, along_y = (x ^ (x >> 1)) & 1, (y ^ (y >> 1)) & 1
+    return core, jnp.where(core == 0, along_x, along_y), jnp.where(core == 0, along_y, along_x)
+
+
 def put_products(ref, core, parts, share, sketched, e_ref, cells=slice(None), add=False):
+    rows = sketched.shape[0]
     for z in range(parts):
         start = pl.multiple_of(window_start(z, share) + SPAN * core, 16)
         part = nt(sketched, e_ref[pl.ds(start, SPAN), cells])
-        for m in range(ref.shape[0]):
-            r, c = m // 2 * 8, m % 2 * 128
-            tile = part[r : r + 8, c : c + 128]
+        for t in range(2):
+            tile = part[:, 128 * t : 128 * t + 128]
             if add:
-                tile = ref[m, 8 * z : 8 * z + 8, :] + tile
-            ref[m, 8 * z : 8 * z + 8, :] = tile
+                tile = ref[t, rows * z : rows * z + rows, :] + tile
+            ref[t, rows * z : rows * z + rows, :] = tile
 
 
 def put_gram(ref, core, parts, gram_ref):
     half = gram_ref[core]
-    for m in range(ref.shape[0]):
-        ref[m, 8 * parts :, :] = half
+    for t in range(2):
+        ref[t, ref.shape[1] - half.shape[0] :, :] = half
 
 
 def begin_kernel(parts, share, s_hbm, e_hbm, theirs_ref, sketched_ref, gram_ref, e_ref, *scratch):
@@ -59,7 +64,7 @@
             copy.start()
             copies.append(copy)
     whole.wait()
-    core = 1 - lax.axis_index("c")
+    core = 1 - place()[0]
     square = None
     for j, block in enumerate(blocks):
         for i, span in enumerate(spans):
@@ -83,7 +88,7 @@
 
 
 def finish_kernel(parts, share, sketched_ref, gram_ref, e_ref, mine_ref):
-    core = lax.axis_index("c")
+    core = place()[0]
     put_gram(mine_ref, core, parts, gram_ref)
     put_products(mine_ref, core, parts, share, sketched_ref[...], e_ref)
 
@@ -96,7 +101,7 @@
         in_specs=[pl.BlockSpec(memory_space=pltpu.HBM)] * 2,
         out_specs=[pl.BlockSpec(memory_space=pltpu.VMEM)] * 4,
         out_shape=[
-            pltpu.VMEM((rows // 4, 8 * parts + rows // 4, 128), jnp.float32),
+            pltpu.VMEM((2, rows * parts + rows // 4, 128), jnp.float32),
             pltpu.VMEM((rows, cells), jnp.bfloat16),
             pltpu.VMEM((2, rows // 4, 128), jnp.float32),
             pltpu.VMEM((genes, cells), jnp.bfloat16),
@@ -106,7 +111,7 @@
             pltpu.VMEM((rows, max(BLOCKS)), jnp.float32),
             pltpu.SemaphoreType.DMA((len(PIECES) * len(BLOCKS) + 1,)),
         ],
-        compiler_params=pltpu.CompilerParams(vmem_limit_bytes=24 << 20),
+        compiler_params=pltpu.CompilerParams(vmem_limit_bytes=16 << 20),
         name="begin",
     )(
         pltpu.with_memory_space_constraint(sketch_map, pltpu.HBM),
@@ -121,11 +126,11 @@
         functools.partial(finish_kernel, parts, genes // parts),
         in_specs=[pl.BlockSpec(memory_space=pltpu.VMEM)] * 3,
         out_specs=pl.BlockSpec(memory_space=pltpu.VMEM),
-        out_shape=pltpu.VMEM((rows // 4, 8 * parts + rows // 4, 128), jnp.float32),
+        out_shape=pltpu.VMEM((2, rows * parts + rows // 4, 128), jnp.float32),
         cost_estimate=pl.CostEstimate(
             flops=rows * genes * cells, bytes_accessed=genes * cells * 2, transcendentals=0
         ),
-        compiler_params=pltpu.CompilerParams(vmem_limit_bytes=24 << 20),
+        compiler_params=pltpu.CompilerParams(vmem_limit_bytes=8 << 20),
         name="finish",
     )(near(sketched), near(gram), near(expression))
 
@@ -187,7 +192,7 @@
 
 
 def factor_kernel(mine_ref, other_ref, out_ref):
-    me = lax.axis_index("c")
+    me = place()[0]
     mine, other = mine_ref[...], other_ref[...]
     halves = [jnp.where(me == 0, mine, other), jnp.where(me == 0, other, mine)]
     sub = lax.broadcasted_iota(jnp.int32, (8, 128), 0)
@@ -202,24 +207,22 @@
         out_ref[8 * g : 8 * g + 8, :] = block[:, :64]
 
 
-def apply_kernel(parts, inverse_ref, in_ref, out_ref):
+def apply_kernel(parts, inverse_ref, mine_ref, other_ref, out_ref):
     rows, share = out_ref.shape
-    genes = jnp.concatenate(
-        [
-            jnp.concatenate([in_ref[(2 * r + h) * 2 + c] for r in range(rows // 8)], axis=0)
-            for c in range(2)
-            for h in range(2)
-        ],
-        axis=1,
-    )
+    core, kept, across = place()
+    mine = [mine_ref[:rows], mine_ref[rows:]]
+    other = [other_ref[:rows], other_ref[rows:]]
+    mine = [jnp.where(kept == t, mine[0], mine[1]) for t in range(2)]
+    other = [jnp.where(across == t, other[0], other[1]) for t in range(2)]
+    tiles = [jnp.where(core == 0, p, q) for p, q in zip(mine + other, other + mine)]
     solved = lax.dot_general(
         inverse_ref[...],
-        genes,
+        jnp.concatenate(tiles, axis=1),
         (((1,), (0,)), ((), ())),
         precision=lax.Precision.HIGHEST,
         preferred_element_type=jnp.float32,
     )
-    extra = lax.axis_index("z") * share % 16
+    extra = lax.axis_index("narrow") * share % 16
     for shift in sorted({z * share % 16 for z in range(parts)}):
 
         @pl.when(extra == shift)
@@ -231,37 +234,72 @@
     return pltpu.with_memory_space_constraint(x, pltpu.VMEM)
 
 
+def wide_index(y, x, core):
+    return (y * 4 + x) * 2 + core
+
+
+def neighbours():
+    return [
+        (wide_index(y, x, core), wide_index(y ^ core, x ^ 1 ^ core, core))
+        for y in range(4)
+        for x in range(4)
+        for core in range(2)
+    ]
+
+
+def holders():
+    return [
+        [wide_index(*((v, u) if core == 0 else (u, v)), core) for v in range(4) for u in (a, 3 - a)]
+        for core in range(2)
+        for a in range(2)
+    ]
+
+
 def on_device(expression, sketch_map):
     rows, genes = sketch_map.shape
-    parts = lax.axis_size("z")
-    swap = [(0, 1), (1, 0)]
+    parts = lax.axis_size("narrow")
+    swap = [(i, i ^ 1) for i in range(lax.axis_size("wide"))]
+    pairs, groups = neighbours(), holders()
+    kept = place()[1]
+    kept, given, sketch_map = lax.optimization_barrier((kept, 1 - kept, sketch_map))
     theirs, sketched, gram, held = begin(sketch_map, expression, parts)
-    theirs = lax.ppermute(theirs, "c", swap)
+    theirs = lax.ppermute(theirs, "wide", swap)
     summed = finish(sketched, gram, held, parts) + theirs
-    total = lax.all_to_all(summed, ("y", "x"), 0, 0, tiled=True).sum(axis=0)
-    ours = total[: 8 * parts].reshape(parts, 8, 128)
-    square = jnp.broadcast_to(total[None, 8 * parts :], (parts, rows // 4, 128))
+    keep = lax.dynamic_slice_in_dim(summed, kept, 1, 0, allow_negative_indices=False)[0]
+    give = lax.dynamic_slice_in_dim(summed, given, 1, 0, allow_negative_indices=False)[0]
+    half = keep + lax.ppermute(give, "wide", pairs)
+    ours = half[: rows * parts].reshape(parts, rows, 128)
+    square = jnp.broadcast_to(half[None, rows * parts :], (parts, rows // 4, 128))
     piece = jnp.concatenate([ours, square], axis=1)
-    piece = lax.all_to_all(piece, "z", 0, 0, tiled=True).sum(axis=0)
-    spread = jnp.broadcast_to(piece[None, :8], (lax.axis_size(WIDE), 8, 128))
-    gathered = near(lax.all_to_all(near(spread), WIDE, 0, 0, tiled=True))
-    square = piece[8:]
-    other = near(lax.ppermute(square, "c", swap))
+    piece = lax.all_to_all(piece, "narrow", 0, 0, tiled=True).sum(axis=0)
+    spread = jnp.broadcast_to(piece[None], (len(groups[0]), *piece.shape))
+    spread = lax.all_to_all(spread, "wide", 0, 0, axis_index_groups=groups, tiled=True)
+    total = spread.sum(axis=0)
+    ours, square = total[:rows], total[rows:]
+    beside = lax.ppermute(ours, "wide", pairs)
     inverse = small(
-        factor_kernel, (rows, rows), "factor", near(square), other, space=pltpu.VMEM
-    )
+        factor_kernel,
+        (rows, rows),
+        "factor",
+        near(square),
+        near(lax.ppermute(square, "wide", swap)),
+        space=pltpu.VMEM,
+    )
+    beside, inverse = lax.optimization_barrier((beside, inverse))
+    mine = jnp.concatenate([ours, beside], axis=0)
+    other = near(lax.ppermute(mine, "wide", swap))
     return small(
         functools.partial(apply_kernel, parts),
         (rows, genes // parts),
         "apply",
         near(inverse),
-        gathered,
+        near(mine),
+        other,
     )
 
 
 def solution(mesh):
-    grid = Mesh(mesh.devices.reshape(4, 4, 2, 8), ("y", "x", "c", "z"))
-    placed = (P(None, ("y", "x", "c", "z")), P())
+    placed = (P(None, ("wide", "narrow")), P())
     return jax.shard_map(
-        on_device, mesh=grid, in_specs=placed, out_specs=P(None, "z"), check_vma=False
-    )
+        on_device, mesh=mesh, in_specs=placed, out_specs=P(None, "narrow"), check_vma=False
+    )

time: 60.8 us -> 59.7 us (0.982)
  waiting for transfers between devices: 4.79 us -> 7.33 us
  blocking collectives: 33.1 us -> 31.6 us
  starting transfers between devices: 9.89 us -> 8.43 us
    ppermute x2 -> x5, waiting for transfers between devices: 0.83 us -> 7.33 us  [the longest x1 5.59 us: on_device(): half = keep + lax.ppermute(give, 'wide', pairs)]
    all_to_all x1 -> x0, starting transfers between devices: 6.12 us -> none  [on_device(): gathered = near(lax.all_to_all(near(spread), WIDE, 0, 0, tiled=True))]
    ppermute x2 -> x5, starting transfers between devices: 3.77 us -> 8.43 us  [the longest x1 4.45 us: on_device(): lax.ppermute(square, 'wide', swap)]
    all_to_all x1 -> x0, waiting for transfers between devices: 3.96 us -> none  [on_device(): gathered = near(lax.all_to_all(near(spread), WIDE, 0, 0, tiled=True))]
    all_to_all x2, blocking collectives: 33.1 us -> 31.6 us  [the longest x1 17.4 us: on_device(): piece = lax.all_to_all(piece, 'narrow', 0, 0, tiled=True).sum(axis=0)]
    broadcast_in_dim x2, local copies, waits for them, and re-layouts: 0.67 us -> 0.03 us  [the longest x1 0.02 us: on_device(): spread = jnp.broadcast_to(piece[None], (len(groups[0]), *piece.shape))]
  transfers between devices with their start and end apart: 3 -> 5, of which waited for: 2 -> 3; matrix products, arithmetic and copies ran while one was open for 0% -> 0% of each run, Pallas kernels for 7% -> 8%
where the time goes in v6:
time: 59.7 us; the launch traced here: 59.5 us
  blocking collectives  31.6 us (53%)
  Pallas kernels  11.8 us (20%)
  starting transfers between devices  8.43 us (14%)
  waiting for transfers between devices  7.33 us (12%)
    all_to_all x1, blocking collectives, on_device(): piece = lax.all_to_all(piece, 'narrow', 0, 0, tiled=True).sum(axis=0)  17.4 us
    all_to_all x1, blocking collectives, on_device(): lax.all_to_all(spread, 'wide', 0, 0, axis_index_groups=groups, tiled=True)  14.1 us
    pallas_call x1, Pallas kernels, begin(): pl.pallas_call(functools.partial(begin_kernel, parts, genes // parts), in...  6.4 us
    ppermute x1, waiting for transfers between devices, on_device(): half = keep + lax.ppermute(give, 'wide', pairs)  5.59 us
    ppermute x1, starting transfers between devices, on_device(): lax.ppermute(square, 'wide', swap)  4.45 us
    pallas_call x2, Pallas kernels, small(): pl.pallas_call(kernel, in_specs=[pl.BlockSpec(memory_space=pltpu.VMEM)] *...  3.44 us
    ppermute x1, starting transfers between devices, on_device(): theirs = lax.ppermute(theirs, 'wide', swap)  3.34 us
    pallas_call x1, Pallas kernels, finish(): pl.pallas_call(functools.partial(finish_kernel, parts, genes // parts), i...  2 us
  transfers between devices with their start and end apart: 5, of which 3 were waited for; matrix products, arithmetic and copies ran while one was open for 0% of the time, Pallas kernels for 8%

profile of v6, /device:TPU:1, one launch (start us, length us, event | category | flops | bytes accessed | tf_op | source)
XLA Modules:
  0.0 59.5 jit_solution(5981566587590671260)
XLA Ops:
  0.0 6.4 %begin.1 = (f32[2,528,128]{2,1,0:T(8,128)S(1)}, bf16[64,1536]{1,0:T(8,128)(2,1)S(1)}, f32[2,16,128]{2,1,0:T(8,128)S(1)}, bf16[4000,1536]{1,0:T(8,128)(2,1)S(1)}) custom-call(bf16[64,4000]{1,0:T(8,128)(2,1)} %s_hbm, bf16[4000,1536]{1,0:T(8,128)(2,1)} %e_hbm.1), custom_call_target="tpu_custom_call" | custom-call | tf_op jit(solution)/shard_map/begin/pallas_call | solution.py:99
  6.4 3.3 %collective-permute-start = (f32[2,528,128]{2,1,0:T(8,128)S(1)}, f32[2,528,128]{2,1,0:T(8,128)S(1)}, u32[]{:S(2)}, u32[]{:S(2)}) collective-permute-start(f32[2,528,128]{2,1,0:T(8,128)S(1)} %get-tuple-element.18), channel_id=1, source_target_pairs={{0,8},{8,0},{16,24},{24,16},{32,40},{40,32},{48,56},{56,48},{64,72... | collective-permute-start | bytes 1622024 | tf_op jit(solution)/shard_map/ppermute | solution.py:266
  9.7 2.0 %finish.1 = f32[2,528,128]{2,1,0:T(8,128)S(1)} custom-call(bf16[64,1536]{1,0:T(8,128)(2,1)S(1)} %get-tuple-element.15.sketched_ref, f32[2,16,128]{2,1,0:T(8,128)S(1)} %get-tuple-element.16.gram_ref, bf16[4000,1536]{1,0:T(8,128)(2,1)S(1)} %get-tuple-element.17.e_ref), custom_call_target="tpu_custom_call" | custom-call | flops 393216000 | bytes 12288000 | tf_op jit(solution)/shard_map/finish/pallas_call | solution.py:125
  11.7 0.0 collective-permute-done
  11.8 0.1 add.6
  11.9 0.1 collective-permute-start.1
  12.0 5.6 %collective-permute-done.1 = f32[528,128]{1,0:T(8,128)S(1)} collective-permute-done((f32[528,128]{1,0:T(8,128)S(1)}, f32[528,128]{1,0:T(8,128)S(1)}, u32[]{:S(2)}, u32[]{:S(2)}) %collective-permute-start.1) | collective-permute-done | bytes 270368 | tf_op jit(solution)/shard_map/ppermute | solution.py:270
  17.7 17.4 %all_to_all.10 = f32[8,80,128]{2,1,0:T(8,128)S(1)} all-to-all(f32[8,80,128]{2,1,0:T(8,128)S(1)} %pad_maximum_fusion), channel_id=1, replica_groups=mesh['wide'=32,'narrow'=8] {'narrow'}, dimensions={0} | all-to-all | bytes 655360 | tf_op jit(solution)/shard_map/all_to_all | solution.py:274
  35.2 14.1 %all_to_all.11 = f32[8,80,128]{2,1,0:T(8,128)S(1)} all-to-all(f32[8,80,128]{2,1,0:T(8,128)S(1)} %broadcast_in_dim.5), channel_id=1, replica_groups={{0,48,64,112,128,176,192,240},{16,32,80,96,144,160,208,224},{8,200,24,2..., dimensions={0} | all-to-all | bytes 655360 | tf_op jit(solution)/shard_map/all_to_all | solution.py:276
  49.3 0.1 collective-permute-start.2
  49.4 4.5 %collective-permute-start.3 = (f32[16,128]{1,0:T(8,128)S(1)}, f32[16,128]{1,0:T(8,128)S(1)}, u32[]{:S(2)}, u32[]{:S(2)}) collective-permute-start(f32[16,128]{1,0:T(8,128)S(1)} %slice.19.mine_ref), channel_id=1, source_target_pairs={{0,8},{8,0},{16,24},{24,16},{32,40},{40,32},{48,56},{56,48},{64,72... | collective-permute-start | bytes 24584 | tf_op jit(solution)/shard_map/ppermute | solution.py:285
  53.9 0.8 %collective-permute-done.3.other_ref = f32[16,128]{1,0:T(8,128)S(1)} collective-permute-done((f32[16,128]{1,0:T(8,128)S(1)}, f32[16,128]{1,0:T(8,128)S(1)}, u32[]{:S(2)}, u32[]{:S(2)}) %collective-permute-start.3) | collective-permute-done | bytes 8224 | tf_op jit(solution)/shard_map/ppermute | solution.py:285
  54.7 2.5 %factor.1.inverse_ref = f32[64,64]{1,0:T(8,128)S(1)} custom-call(f32[16,128]{1,0:T(8,128)S(1)} %slice.19.mine_ref, f32[16,128]{1,0:T(8,128)S(1)} %collective-permute-done.3.other_ref), custom_call_target="tpu_custom_call" | custom-call | tf_op jit(solution)/shard_map/factor/pallas_call | solution.py:139
  57.2 0.0 collective-permute-done.2
  57.2 0.5 collective-permute-start.4
  57.7 0.9 %collective-permute-done.4.other_ref = f32[128,128]{1,0:T(8,128)S(1)} collective-permute-done((f32[128,128]{1,0:T(8,128)S(1)}, f32[128,128]{1,0:T(8,128)S(1)}, u32[]{:S(2)}, u32[]{:S(2)}) %collective-permute-start.4) | collective-permute-done | bytes 65568 | tf_op jit(solution)/shard_map/ppermute | solution.py:290
  58.6 0.9 %apply.1 = f32[64,500]{1,0:T(8,128)} custom-call(f32[64,64]{1,0:T(8,128)S(1)} %factor.1.inverse_ref, f32[128,128]{1,0:T(8,128)S(1)} %pad_maximum_fusion.1.mine_ref, f32[128,128]{1,0:T(8,128)S(1)} %collective-permute-done.4.other_ref), custom_call_target="tpu_custom_call" | custom-call | tf_op jit(solution)/shard_map/apply/pallas_call | solution.py:139
  (12 shorter events, 0.2 us)
Async XLA Ops:
  6.4 5.3 %collective-permute-start = (f32[2,528,128]{2,1,0:T(8,128)S(1)}, f32[2,528,128]{2,1,0:T(8,128)S(1)}, u32[]{:S(2)}, u32[]{:S(2)}) collective-permute-start(f32[2,528,128]{2,1,0:T(8,128)S(1)} %get-tuple-element.18), channel_id=1, source_target_pairs={{0,8},{8,0},{16,24},{24,16},{32,40},{40,32},{48,56},{56,48},{64,72... | collective-permute-start | bytes 1622024 | tf_op jit(solution)/shard_map/ppermute | solution.py:266
  11.9 5.7 %collective-permute-start.1 = (f32[528,128]{1,0:T(8,128)S(1)}, f32[528,128]{1,0:T(8,128)S(1)}, u32[]{:S(2)}, u32[]{:S(2)}) collective-permute-start(f32[528,128]{1,0:T(8,128)S(1)} %dynamic-slice_bitcast_fusion), channel_id=1, source_target_pairs={{0,16},{8,72},{16,0},{24,88},{32,48},{40,104},{48,32},{56,120},{64... | collective-permute-start | bytes 811016 | tf_op jit(solution)/shard_map/ppermute | solution.py:270
  49.3 7.9 %collective-permute-start.2 = (f32[64,128]{1,0:T(8,128)S(1)}, f32[64,128]{1,0:T(8,128)S(1)}, u32[]{:S(2)}, u32[]{:S(2)}) collective-permute-start(f32[64,128]{1,0:T(8,128)S(1)} %slice.18), channel_id=1, source_target_pairs={{0,16},{8,72},{16,0},{24,88},{32,48},{40,104},{48,32},{56,120},{64... | collective-permute-start | bytes 98312 | tf_op jit(solution)/shard_map/ppermute | solution.py:279
  49.4 5.3 %collective-permute-start.3 = (f32[16,128]{1,0:T(8,128)S(1)}, f32[16,128]{1,0:T(8,128)S(1)}, u32[]{:S(2)}, u32[]{:S(2)}) collective-permute-start(f32[16,128]{1,0:T(8,128)S(1)} %slice.19.mine_ref), channel_id=1, source_target_pairs={{0,8},{8,0},{16,24},{24,16},{32,40},{40,32},{48,56},{56,48},{64,72... | collective-permute-start | bytes 24584 | tf_op jit(solution)/shard_map/ppermute | solution.py:285
  57.2 1.4 %collective-permute-start.4 = (f32[128,128]{1,0:T(8,128)S(1)}, f32[128,128]{1,0:T(8,128)S(1)}, u32[]{:S(2)}, u32[]{:S(2)}) collective-permute-start(f32[128,128]{1,0:T(8,128)S(1)} %pad_maximum_fusion.1.mine_ref), channel_id=1, source_target_pairs={{0,8},{8,0},{16,24},{24,16},{32,40},{40,32},{48,56},{56,48},{64,72... | collective-permute-start | bytes 196616 | tf_op jit(solution)/shard_map/ppermute | solution.py:290

commit v7 on v6

--- a/solution.py
+++ b/solution.py
@@ -31,22 +31,19 @@
     return core, jnp.where(core == 0, along_x, along_y), jnp.where(core == 0, along_y, along_x)
 
 
-def put_products(ref, core, parts, share, sketched, e_ref, cells=slice(None), add=False):
+def put_products(ref, core, half, parts, share, sketched, e_ref, cells=slice(None), add=False):
     rows = sketched.shape[0]
     for z in range(parts):
-        start = pl.multiple_of(window_start(z, share) + SPAN * core, 16)
-        part = nt(sketched, e_ref[pl.ds(start, SPAN), cells])
-        for t in range(2):
-            tile = part[:, 128 * t : 128 * t + 128]
-            if add:
-                tile = ref[t, rows * z : rows * z + rows, :] + tile
-            ref[t, rows * z : rows * z + rows, :] = tile
-
-
-def put_gram(ref, core, parts, gram_ref):
+        start = pl.multiple_of(window_start(z, share) + SPAN * core + SPAN // 2 * half, 16)
+        tile = nt(sketched, e_ref[pl.ds(start, SPAN // 2), cells])
+        if add:
+            tile = ref[rows * z : rows * z + rows, :] + tile
+        ref[rows * z : rows * z + rows, :] = tile
+
+
+def put_gram(ref, core, gram_ref):
     half = gram_ref[core]
-    for t in range(2):
-        ref[t, ref.shape[1] - half.shape[0] :, :] = half
+    ref[ref.shape[0] - half.shape[0] :, :] = half
 
 
 def begin_kernel(parts, share, s_hbm, e_hbm, theirs_ref, sketched_ref, gram_ref, e_ref, *scratch):
@@ -64,7 +61,8 @@
             copy.start()
             copies.append(copy)
     whole.wait()
-    core = 1 - place()[0]
+    core, _, half = place()
+    core, half = 1 - core, 1 - half
     square = None
     for j, block in enumerate(blocks):
         for i, span in enumerate(spans):
@@ -78,19 +76,20 @@
         sketched_ref[:, block] = sketched
         term = nt(sketched, sketched)
         square = term if j == 0 else square + term
-        put_products(theirs_ref, core, parts, share, sketched, e_ref, block, j > 0)
+        put_products(theirs_ref, core, half, parts, share, sketched, e_ref, block, j > 0)
     quarter = square.shape[0] // 4
     for h in range(2):
         top = square[2 * quarter * h : 2 * quarter * h + quarter]
         low = square[2 * quarter * h + quarter : 2 * quarter * (h + 1)]
         gram_ref[h] = jnp.concatenate([top, low], axis=1)
-    put_gram(theirs_ref, core, parts, gram_ref)
-
-
-def finish_kernel(parts, share, sketched_ref, gram_ref, e_ref, mine_ref):
-    core = place()[0]
-    put_gram(mine_ref, core, parts, gram_ref)
-    put_products(mine_ref, core, parts, share, sketched_ref[...], e_ref)
+    put_gram(theirs_ref, core, gram_ref)
+
+
+def more_kernel(which, parts, share, sketched_ref, gram_ref, e_ref, out_ref):
+    core, kept, across = place()
+    core, half = {"give": (core, 1 - kept), "keep": (core, kept), "theirs": (1 - core, across)}[which]
+    put_gram(out_ref, core, gram_ref)
+    put_products(out_ref, core, half, parts, share, sketched_ref[...], e_ref)
 
 
 def begin(sketch_map, expression, parts):
@@ -101,7 +100,7 @@
         in_specs=[pl.BlockSpec(memory_space=pltpu.HBM)] * 2,
         out_specs=[pl.BlockSpec(memory_space=pltpu.VMEM)] * 4,
         out_shape=[
-            pltpu.VMEM((2, rows * parts + rows // 4, 128), jnp.float32),
+            pltpu.VMEM((rows * parts + rows // 4, 128), jnp.float32),
             pltpu.VMEM((rows, cells), jnp.bfloat16),
             pltpu.VMEM((2, rows // 4, 128), jnp.float32),
             pltpu.VMEM((genes, cells), jnp.bfloat16),
@@ -119,19 +118,19 @@
     )
 
 
-def finish(sketched, gram, expression, parts):
+def more(which, sketched, gram, expression, parts):
     genes, cells = expression.shape
     rows = sketched.shape[0]
     return pl.pallas_call(
-        functools.partial(finish_kernel, parts, genes // parts),
+        functools.partial(more_kernel, which, parts, genes // parts),
         in_specs=[pl.BlockSpec(memory_space=pltpu.VMEM)] * 3,
         out_specs=pl.BlockSpec(memory_space=pltpu.VMEM),
-        out_shape=pltpu.VMEM((2, rows * parts + rows // 4, 128), jnp.float32),
+        out_shape=pltpu.VMEM((rows * parts + rows // 4, 128), jnp.float32),
         cost_estimate=pl.CostEstimate(
-            flops=rows * genes * cells, bytes_accessed=genes * cells * 2, transcendentals=0
+            flops=rows * genes * cells // 2, bytes_accessed=genes * cells, transcendentals=0
         ),
         compiler_params=pltpu.CompilerParams(vmem_limit_bytes=8 << 20),
-        name="finish",
+        name=which,
     )(near(sketched), near(gram), near(expression))
 
 
@@ -260,14 +259,13 @@
     parts = lax.axis_size("narrow")
     swap = [(i, i ^ 1) for i in range(lax.axis_size("wide"))]
     pairs, groups = neighbours(), holders()
-    kept = place()[1]
-    kept, given, sketch_map = lax.optimization_barrier((kept, 1 - kept, sketch_map))
     theirs, sketched, gram, held = begin(sketch_map, expression, parts)
     theirs = lax.ppermute(theirs, "wide", swap)
-    summed = finish(sketched, gram, held, parts) + theirs
-    keep = lax.dynamic_slice_in_dim(summed, kept, 1, 0, allow_negative_indices=False)[0]
-    give = lax.dynamic_slice_in_dim(summed, given, 1, 0, allow_negative_indices=False)[0]
-    half = keep + lax.ppermute(give, "wide", pairs)
+    give = more("give", sketched, gram, held, parts) + theirs
+    give, gram = lax.optimization_barrier((give, gram))
+    given = lax.ppermute(give, "wide", pairs)
+    theirs = lax.ppermute(more("theirs", sketched, gram, held, parts), "wide", swap)
+    half = more("keep", sketched, gram, held, parts) + theirs + given
     ours = half[: rows * parts].reshape(parts, rows, 128)
     square = jnp.broadcast_to(half[None, rows * parts :], (parts, rows // 4, 128))
     piece = jnp.concatenate([ours, square], axis=1)

time: 59.7 us -> 59.7 us (level)
  waiting for transfers between devices: 7.33 us -> 6.15 us
  Pallas kernels: 11.8 us -> 12.7 us
    pallas_call x1 -> x3, Pallas kernels: 2 us -> 3.52 us  [more(): pl.pallas_call(functools.partial(more_kernel, which, parts, genes // part...]
    ppermute x1 -> x2, waiting for transfers between devices: 5.59 us -> 4.42 us  [the longest x1 4.41 us: on_device(): given = lax.ppermute(give, 'wide', pairs)]
    pallas_call x1, Pallas kernels: 6.4 us -> 5.72 us  [begin(): pl.pallas_call(functools.partial(begin_kernel, parts, genes // parts), in...]
  transfers between devices with their start and end apart: 5 -> 6, of which waited for: 3 -> 3; matrix products, arithmetic and copies ran while one was open for 0% -> 0% of each run, Pallas kernels for 8% -> 8%
where the time goes in v7:
time: 59.7 us; the launch traced here: 59.5 us
  blocking collectives  31.5 us (53%)
  Pallas kernels  12.7 us (21%)
  starting transfers between devices  8.87 us (15%)
  waiting for transfers between devices  6.15 us (10%)
    all_to_all x1, blocking collectives, on_device(): piece = lax.all_to_all(piece, 'narrow', 0, 0, tiled=True).sum(axis=0)  17.4 us
    all_to_all x1, blocking collectives, on_device(): lax.all_to_all(spread, 'wide', 0, 0, axis_index_groups=groups, tiled=True)  14.1 us
    pallas_call x1, Pallas kernels, begin(): pl.pallas_call(functools.partial(begin_kernel, parts, genes // parts), in...  5.72 us
    ppermute x1, starting transfers between devices, on_device(): lax.ppermute(square, 'wide', swap)  4.54 us
    ppermute x1, waiting for transfers between devices, on_device(): given = lax.ppermute(give, 'wide', pairs)  4.41 us
    pallas_call x3, Pallas kernels, more(): pl.pallas_call(functools.partial(more_kernel, which, parts, genes // part...  3.52 us
    pallas_call x2, Pallas kernels, small(): pl.pallas_call(kernel, in_specs=[pl.BlockSpec(memory_space=pltpu.VMEM)] *...  3.44 us
    ppermute x1, starting transfers between devices, on_device(): theirs = lax.ppermute(theirs, 'wide', swap)  3.33 us
  transfers between devices with their start and end apart: 6, of which 3 were waited for; matrix products, arithmetic and copies ran while one was open for 0% of the time, Pallas kernels for 8%

profile of v7, /device:TPU:1, one launch (start us, length us, event | category | flops | bytes accessed | tf_op | source)
XLA Modules:
  0.0 59.5 jit_solution(4443905838116225544)
XLA Ops:
  0.0 5.7 %begin.1 = (f32[528,128]{1,0:T(8,128)S(1)}, bf16[64,1536]{1,0:T(8,128)(2,1)S(1)}, f32[2,16,128]{2,1,0:T(8,128)S(1)}, bf16[4000,1536]{1,0:T(8,128)(2,1)S(1)}) custom-call(bf16[64,4000]{1,0:T(8,128)(2,1)} %s_hbm.1, bf16[4000,1536]{1,0:T(8,128)(2,1)} %e_hbm.1), custom_call_target="tpu_custom_call" | custom-call | tf_op jit(solution)/shard_map/begin/pallas_call | solution.py:98
  5.7 3.3 %collective-permute-start = (f32[528,128]{1,0:T(8,128)S(1)}, f32[528,128]{1,0:T(8,128)S(1)}, u32[]{:S(2)}, u32[]{:S(2)}) collective-permute-start(f32[528,128]{1,0:T(8,128)S(1)} %get-tuple-element.16), channel_id=1, source_target_pairs={{0,8},{8,0},{16,24},{24,16},{32,40},{40,32},{48,56},{56,48},{64,72... | collective-permute-start | bytes 811016 | tf_op jit(solution)/shard_map/ppermute | solution.py:263
  9.1 1.2 %give.1 = f32[528,128]{1,0:T(8,128)S(1)} custom-call(bf16[64,1536]{1,0:T(8,128)(2,1)S(1)} %get-tuple-element.13.sketched_ref, f32[2,16,128]{2,1,0:T(8,128)S(1)} %get-tuple-element.17.gram_ref, bf16[4000,1536]{1,0:T(8,128)(2,1)S(1)} %get-tuple-element.15.e_ref), custom_call_target="tpu_custom_call" | custom-call | flops 196608000 | bytes 6144000 | tf_op jit(solution)/shard_map/give/pallas_call | solution.py:124
  10.2 0.0 collective-permute-done
  10.3 1.2 %theirs.1 = f32[528,128]{1,0:T(8,128)S(1)} custom-call(bf16[64,1536]{1,0:T(8,128)(2,1)S(1)} %get-tuple-element.13.sketched_ref, f32[2,16,128]{2,1,0:T(8,128)S(1)} %get-tuple-element.17.gram_ref, bf16[4000,1536]{1,0:T(8,128)(2,1)S(1)} %get-tuple-element.15.e_ref), custom_call_target="tpu_custom_call" | custom-call | flops 196608000 | bytes 6144000 | tf_op jit(solution)/shard_map/theirs/pallas_call | solution.py:124
  11.5 0.4 collective-permute-start.1
  11.9 0.0 collective-permute-start.2
  11.9 1.2 %keep.1 = f32[528,128]{1,0:T(8,128)S(1)} custom-call(bf16[64,1536]{1,0:T(8,128)(2,1)S(1)} %get-tuple-element.13.sketched_ref, f32[2,16,128]{2,1,0:T(8,128)S(1)} %get-tuple-element.17.gram_ref, bf16[4000,1536]{1,0:T(8,128)(2,1)S(1)} %get-tuple-element.15.e_ref), custom_call_target="tpu_custom_call" | custom-call | flops 196608000 | bytes 6144000 | tf_op jit(solution)/shard_map/keep/pallas_call | solution.py:124
  13.1 0.0 collective-permute-done.1
  13.1 4.4 %collective-permute-done.2 = f32[528,128]{1,0:T(8,128)S(1)} collective-permute-done((f32[528,128]{1,0:T(8,128)S(1)}, f32[528,128]{1,0:T(8,128)S(1)}, u32[]{:S(2)}, u32[]{:S(2)}) %collective-permute-start.2) | collective-permute-done | bytes 270368 | tf_op jit(solution)/shard_map/ppermute | solution.py:266
  17.5 0.1 add_add_fusion
  17.7 17.4 %all_to_all.10 = f32[8,80,128]{2,1,0:T(8,128)S(1)} all-to-all(f32[8,80,128]{2,1,0:T(8,128)S(1)} %pad_maximum_fusion), channel_id=1, replica_groups=mesh['wide'=32,'narrow'=8] {'narrow'}, dimensions={0} | all-to-all | bytes 655360 | tf_op jit(solution)/shard_map/all_to_all | solution.py:272
  35.1 14.1 %all_to_all.11 = f32[8,80,128]{2,1,0:T(8,128)S(1)} all-to-all(f32[8,80,128]{2,1,0:T(8,128)S(1)} %broadcast_in_dim.5), channel_id=1, replica_groups={{0,48,64,112,128,176,192,240},{16,32,80,96,144,160,208,224},{8,200,24,2..., dimensions={0} | all-to-all | bytes 655360 | tf_op jit(solution)/shard_map/all_to_all | solution.py:274
  49.2 0.1 collective-permute-start.3
  49.3 4.5 %collective-permute-start.4 = (f32[16,128]{1,0:T(8,128)S(1)}, f32[16,128]{1,0:T(8,128)S(1)}, u32[]{:S(2)}, u32[]{:S(2)}) collective-permute-start(f32[16,128]{1,0:T(8,128)S(1)} %slice.19.mine_ref), channel_id=1, source_target_pairs={{0,8},{8,0},{16,24},{24,16},{32,40},{40,32},{48,56},{56,48},{64,72... | collective-permute-start | bytes 24584 | tf_op jit(solution)/shard_map/ppermute | solution.py:283
  53.9 0.8 %collective-permute-done.4.other_ref = f32[16,128]{1,0:T(8,128)S(1)} collective-permute-done((f32[16,128]{1,0:T(8,128)S(1)}, f32[16,128]{1,0:T(8,128)S(1)}, u32[]{:S(2)}, u32[]{:S(2)}) %collective-permute-start.4) | collective-permute-done | bytes 8224 | tf_op jit(solution)/shard_map/ppermute | solution.py:283
  54.7 2.5 %factor.1.inverse_ref = f32[64,64]{1,0:T(8,128)S(1)} custom-call(f32[16,128]{1,0:T(8,128)S(1)} %slice.19.mine_ref, f32[16,128]{1,0:T(8,128)S(1)} %collective-permute-done.4.other_ref), custom_call_target="tpu_custom_call" | custom-call | tf_op jit(solution)/shard_map/factor/pallas_call | solution.py:138
  57.2 0.0 collective-permute-done.3
  57.2 0.5 collective-permute-start.5
  57.7 0.9 %collective-permute-done.5.other_ref = f32[128,128]{1,0:T(8,128)S(1)} collective-permute-done((f32[128,128]{1,0:T(8,128)S(1)}, f32[128,128]{1,0:T(8,128)S(1)}, u32[]{:S(2)}, u32[]{:S(2)}) %collective-permute-start.5) | collective-permute-done | bytes 65568 | tf_op jit(solution)/shard_map/ppermute | solution.py:288
  58.6 0.9 %apply.1 = f32[64,500]{1,0:T(8,128)} custom-call(f32[64,64]{1,0:T(8,128)S(1)} %factor.1.inverse_ref, f32[128,128]{1,0:T(8,128)S(1)} %pad_maximum_fusion.1.mine_ref, f32[128,128]{1,0:T(8,128)S(1)} %collective-permute-done.5.other_ref), custom_call_target="tpu_custom_call" | custom-call | tf_op jit(solution)/shard_map/apply/pallas_call | solution.py:138
  (11 shorter events, 0.2 us)
Async XLA Ops:
  5.7 4.5 %collective-permute-start = (f32[528,128]{1,0:T(8,128)S(1)}, f32[528,128]{1,0:T(8,128)S(1)}, u32[]{:S(2)}, u32[]{:S(2)}) collective-permute-start(f32[528,128]{1,0:T(8,128)S(1)} %get-tuple-element.16), channel_id=1, source_target_pairs={{0,8},{8,0},{16,24},{24,16},{32,40},{40,32},{48,56},{56,48},{64,72... | collective-permute-start | bytes 811016 | tf_op jit(solution)/shard_map/ppermute | solution.py:263
  11.5 1.6 %collective-permute-start.1 = (f32[528,128]{1,0:T(8,128)S(1)}, f32[528,128]{1,0:T(8,128)S(1)}, u32[]{:S(2)}, u32[]{:S(2)}) collective-permute-start(f32[528,128]{1,0:T(8,128)S(1)} %theirs.1), channel_id=1, source_target_pairs={{0,8},{8,0},{16,24},{24,16},{32,40},{40,32},{48,56},{56,48},{64,72... | collective-permute-start | bytes 811016 | tf_op jit(solution)/shard_map/ppermute | solution.py:267
  11.9 5.6 %collective-permute-start.2 = (f32[528,128]{1,0:T(8,128)S(1)}, f32[528,128]{1,0:T(8,128)S(1)}, u32[]{:S(2)}, u32[]{:S(2)}) collective-permute-start(f32[528,128]{1,0:T(8,128)S(1)} %add.9), channel_id=1, source_target_pairs={{0,16},{8,72},{16,0},{24,88},{32,48},{40,104},{48,32},{56,120},{64... | collective-permute-start | bytes 811016 | tf_op jit(solution)/shard_map/ppermute | solution.py:266
  49.2 8.0 %collective-permute-start.3 = (f32[64,128]{1,0:T(8,128)S(1)}, f32[64,128]{1,0:T(8,128)S(1)}, u32[]{:S(2)}, u32[]{:S(2)}) collective-permute-start(f32[64,128]{1,0:T(8,128)S(1)} %slice.18), channel_id=1, source_target_pairs={{0,16},{8,72},{16,0},{24,88},{32,48},{40,104},{48,32},{56,120},{64... | collective-permute-start | bytes 98312 | tf_op jit(solution)/shard_map/ppermute | solution.py:277
  49.3 5.4 %collective-permute-start.4 = (f32[16,128]{1,0:T(8,128)S(1)}, f32[16,128]{1,0:T(8,128)S(1)}, u32[]{:S(2)}, u32[]{:S(2)}) collective-permute-start(f32[16,128]{1,0:T(8,128)S(1)} %slice.19.mine_ref), channel_id=1, source_target_pairs={{0,8},{8,0},{16,24},{24,16},{32,40},{40,32},{48,56},{56,48},{64,72... | collective-permute-start | bytes 24584 | tf_op jit(solution)/shard_map/ppermute | solution.py:283
  57.2 1.4 %collective-permute-start.5 = (f32[128,128]{1,0:T(8,128)S(1)}, f32[128,128]{1,0:T(8,128)S(1)}, u32[]{:S(2)}, u32[]{:S(2)}) collective-permute-start(f32[128,128]{1,0:T(8,128)S(1)} %pad_maximum_fusion.1.mine_ref), channel_id=1, source_target_pairs={{0,8},{8,0},{16,24},{24,16},{32,40},{40,32},{48,56},{56,48},{64,72... | collective-permute-start | bytes 196616 | tf_op jit(solution)/shard_map/ppermute | solution.py:288

commit v8 on v7

--- a/solution.py
+++ b/solution.py
@@ -265,7 +265,8 @@
     give, gram = lax.optimization_barrier((give, gram))
     given = lax.ppermute(give, "wide", pairs)
     theirs = lax.ppermute(more("theirs", sketched, gram, held, parts), "wide", swap)
-    half = more("keep", sketched, gram, held, parts) + theirs + given
+    keep = lax.optimization_barrier(more("keep", sketched, gram, held, parts) + given)
+    half = keep + theirs
     ours = half[: rows * parts].reshape(parts, rows, 128)
     square = jnp.broadcast_to(half[None, rows * parts :], (parts, rows // 4, 128))
     piece = jnp.concatenate([ours, square], axis=1)

time: 59.7 us -> 58.2 us (0.975)
  waiting for transfers between devices: 6.15 us -> 4.52 us
    ppermute x1, waiting for transfers between devices: 4.41 us -> 2.78 us  [on_device(): given = lax.ppermute(give, 'wide', pairs)]
  transfers between devices with their start and end apart: 6 -> 6, of which waited for: 3 -> 3; matrix products, arithmetic and copies ran while one was open for 0% -> 0% of each run, Pallas kernels for 8% -> 10%
where the time goes in v8:
time: 58.2 us; the launch traced here: 58 us
  blocking collectives  31.2 us (54%)
  Pallas kernels  12.7 us (22%)
  starting transfers between devices  9.18 us (16%)
  waiting for transfers between devices  4.52 us (8%)
    all_to_all x1, blocking collectives, on_device(): piece = lax.all_to_all(piece, 'narrow', 0, 0, tiled=True).sum(axis=0)  17.3 us
    all_to_all x1, blocking collectives, on_device(): lax.all_to_all(spread, 'wide', 0, 0, axis_index_groups=groups, tiled=True)  14 us
    pallas_call x1, Pallas kernels, begin(): pl.pallas_call(functools.partial(begin_kernel, parts, genes // parts), in...  5.72 us
    ppermute x1, starting transfers between devices, on_device(): lax.ppermute(square, 'wide', swap)  4.77 us
    pallas_call x3, Pallas kernels, more(): pl.pallas_call(functools.partial(more_kernel, which, parts, genes // part...  3.52 us
    pallas_call x2, Pallas kernels, small(): pl.pallas_call(kernel, in_specs=[pl.BlockSpec(memory_space=pltpu.VMEM)] *...  3.44 us
    ppermute x1, starting transfers between devices, on_device(): theirs = lax.ppermute(theirs, 'wide', swap)  3.33 us
    ppermute x1, waiting for transfers between devices, on_device(): given = lax.ppermute(give, 'wide', pairs)  2.78 us
  transfers between devices with their start and end apart: 6, of which 3 were waited for; matrix products, arithmetic and copies ran while one was open for 0% of the time, Pallas kernels for 10%

profile of v8, /device:TPU:1, one launch (start us, length us, event | category | flops | bytes accessed | tf_op | source)
XLA Modules:
  0.0 58.0 jit_solution(11655902609103495275)
XLA Ops:
  0.0 5.7 %begin.1 = (f32[528,128]{1,0:T(8,128)S(1)}, bf16[64,1536]{1,0:T(8,128)(2,1)S(1)}, f32[2,16,128]{2,1,0:T(8,128)S(1)}, bf16[4000,1536]{1,0:T(8,128)(2,1)S(1)}) custom-call(bf16[64,4000]{1,0:T(8,128)(2,1)} %s_hbm.1, bf16[4000,1536]{1,0:T(8,128)(2,1)} %e_hbm.1), custom_call_target="tpu_custom_call" | custom-call | tf_op jit(solution)/shard_map/begin/pallas_call | solution.py:98
  5.7 3.3 %collective-permute-start = (f32[528,128]{1,0:T(8,128)S(1)}, f32[528,128]{1,0:T(8,128)S(1)}, u32[]{:S(2)}, u32[]{:S(2)}) collective-permute-start(f32[528,128]{1,0:T(8,128)S(1)} %get-tuple-element.16), channel_id=1, source_target_pairs={{0,8},{8,0},{16,24},{24,16},{32,40},{40,32},{48,56},{56,48},{64,72... | collective-permute-start | bytes 811016 | tf_op jit(solution)/shard_map/ppermute | solution.py:263
  9.1 1.2 %give.1 = f32[528,128]{1,0:T(8,128)S(1)} custom-call(bf16[64,1536]{1,0:T(8,128)(2,1)S(1)} %get-tuple-element.13.sketched_ref, f32[2,16,128]{2,1,0:T(8,128)S(1)} %get-tuple-element.17.gram_ref, bf16[4000,1536]{1,0:T(8,128)(2,1)S(1)} %get-tuple-element.15.e_ref), custom_call_target="tpu_custom_call" | custom-call | flops 196608000 | bytes 6144000 | tf_op jit(solution)/shard_map/give/pallas_call | solution.py:124
  10.2 0.0 collective-permute-done
  10.3 0.1 collective-permute-start.1
  10.4 1.2 %theirs.1 = f32[528,128]{1,0:T(8,128)S(1)} custom-call(bf16[64,1536]{1,0:T(8,128)(2,1)S(1)} %get-tuple-element.13.sketched_ref, f32[2,16,128]{2,1,0:T(8,128)S(1)} %get-tuple-element.17.gram_ref, bf16[4000,1536]{1,0:T(8,128)(2,1)S(1)} %get-tuple-element.15.e_ref), custom_call_target="tpu_custom_call" | custom-call | flops 196608000 | bytes 6144000 | tf_op jit(solution)/shard_map/theirs/pallas_call | solution.py:124
  11.6 0.4 collective-permute-start.2
  12.0 1.2 %keep.1 = f32[528,128]{1,0:T(8,128)S(1)} custom-call(bf16[64,1536]{1,0:T(8,128)(2,1)S(1)} %get-tuple-element.13.sketched_ref, f32[2,16,128]{2,1,0:T(8,128)S(1)} %get-tuple-element.17.gram_ref, bf16[4000,1536]{1,0:T(8,128)(2,1)S(1)} %get-tuple-element.15.e_ref), custom_call_target="tpu_custom_call" | custom-call | flops 196608000 | bytes 6144000 | tf_op jit(solution)/shard_map/keep/pallas_call | solution.py:124
  13.2 2.8 %collective-permute-done.1 = f32[528,128]{1,0:T(8,128)S(1)} collective-permute-done((f32[528,128]{1,0:T(8,128)S(1)}, f32[528,128]{1,0:T(8,128)S(1)}, u32[]{:S(2)}, u32[]{:S(2)}) %collective-permute-start.1) | collective-permute-done | bytes 270368 | tf_op jit(solution)/shard_map/ppermute | solution.py:266
  16.0 0.0 collective-permute-done.2
  16.1 17.3 %all_to_all.10 = f32[8,80,128]{2,1,0:T(8,128)S(1)} all-to-all(f32[8,80,128]{2,1,0:T(8,128)S(1)} %pad_maximum_fusion), channel_id=1, replica_groups=mesh['wide'=32,'narrow'=8] {'narrow'}, dimensions={0} | all-to-all | bytes 655360 | tf_op jit(solution)/shard_map/all_to_all | solution.py:273
  33.5 14.0 %all_to_all.11 = f32[8,80,128]{2,1,0:T(8,128)S(1)} all-to-all(f32[8,80,128]{2,1,0:T(8,128)S(1)} %broadcast_in_dim.5), channel_id=1, replica_groups={{0,48,64,112,128,176,192,240},{16,32,80,96,144,160,208,224},{8,200,24,2..., dimensions={0} | all-to-all | bytes 655360 | tf_op jit(solution)/shard_map/all_to_all | solution.py:275
  47.5 0.1 collective-permute-start.3
  47.6 4.8 %collective-permute-start.4 = (f32[16,128]{1,0:T(8,128)S(1)}, f32[16,128]{1,0:T(8,128)S(1)}, u32[]{:S(2)}, u32[]{:S(2)}) collective-permute-start(f32[16,128]{1,0:T(8,128)S(1)} %slice.19.mine_ref), channel_id=1, source_target_pairs={{0,8},{8,0},{16,24},{24,16},{32,40},{40,32},{48,56},{56,48},{64,72... | collective-permute-start | bytes 24584 | tf_op jit(solution)/shard_map/ppermute | solution.py:284
  52.4 0.8 %collective-permute-done.4.other_ref = f32[16,128]{1,0:T(8,128)S(1)} collective-permute-done((f32[16,128]{1,0:T(8,128)S(1)}, f32[16,128]{1,0:T(8,128)S(1)}, u32[]{:S(2)}, u32[]{:S(2)}) %collective-permute-start.4) | collective-permute-done | bytes 8224 | tf_op jit(solution)/shard_map/ppermute | solution.py:284
  53.2 2.5 %factor.1.inverse_ref = f32[64,64]{1,0:T(8,128)S(1)} custom-call(f32[16,128]{1,0:T(8,128)S(1)} %slice.19.mine_ref, f32[16,128]{1,0:T(8,128)S(1)} %collective-permute-done.4.other_ref), custom_call_target="tpu_custom_call" | custom-call | tf_op jit(solution)/shard_map/factor/pallas_call | solution.py:138
  55.7 0.0 collective-permute-done.3
  55.7 0.5 collective-permute-start.5
  56.2 0.9 %collective-permute-done.5.other_ref = f32[128,128]{1,0:T(8,128)S(1)} collective-permute-done((f32[128,128]{1,0:T(8,128)S(1)}, f32[128,128]{1,0:T(8,128)S(1)}, u32[]{:S(2)}, u32[]{:S(2)}) %collective-permute-start.5) | collective-permute-done | bytes 65568 | tf_op jit(solution)/shard_map/ppermute | solution.py:289
  57.1 0.9 %apply.1 = f32[64,500]{1,0:T(8,128)} custom-call(f32[64,64]{1,0:T(8,128)S(1)} %factor.1.inverse_ref, f32[128,128]{1,0:T(8,128)S(1)} %pad_maximum_fusion.1.mine_ref, f32[128,128]{1,0:T(8,128)S(1)} %collective-permute-done.5.other_ref), custom_call_target="tpu_custom_call" | custom-call | tf_op jit(solution)/shard_map/apply/pallas_call | solution.py:138
  (13 shorter events, 0.2 us)
Async XLA Ops:
  5.7 4.5 %collective-permute-start = (f32[528,128]{1,0:T(8,128)S(1)}, f32[528,128]{1,0:T(8,128)S(1)}, u32[]{:S(2)}, u32[]{:S(2)}) collective-permute-start(f32[528,128]{1,0:T(8,128)S(1)} %get-tuple-element.16), channel_id=1, source_target_pairs={{0,8},{8,0},{16,24},{24,16},{32,40},{40,32},{48,56},{56,48},{64,72... | collective-permute-start | bytes 811016 | tf_op jit(solution)/shard_map/ppermute | solution.py:263
  10.3 5.7 %collective-permute-start.1 = (f32[528,128]{1,0:T(8,128)S(1)}, f32[528,128]{1,0:T(8,128)S(1)}, u32[]{:S(2)}, u32[]{:S(2)}) collective-permute-start(f32[528,128]{1,0:T(8,128)S(1)} %add.9), channel_id=1, source_target_pairs={{0,16},{8,72},{16,0},{24,88},{32,48},{40,104},{48,32},{56,120},{64... | collective-permute-start | bytes 811016 | tf_op jit(solution)/shard_map/ppermute | solution.py:266
  11.6 4.4 %collective-permute-start.2 = (f32[528,128]{1,0:T(8,128)S(1)}, f32[528,128]{1,0:T(8,128)S(1)}, u32[]{:S(2)}, u32[]{:S(2)}) collective-permute-start(f32[528,128]{1,0:T(8,128)S(1)} %theirs.1), channel_id=1, source_target_pairs={{0,8},{8,0},{16,24},{24,16},{32,40},{40,32},{48,56},{56,48},{64,72... | collective-permute-start | bytes 811016 | tf_op jit(solution)/shard_map/ppermute | solution.py:267
  47.5 8.2 %collective-permute-start.3 = (f32[64,128]{1,0:T(8,128)S(1)}, f32[64,128]{1,0:T(8,128)S(1)}, u32[]{:S(2)}, u32[]{:S(2)}) collective-permute-start(f32[64,128]{1,0:T(8,128)S(1)} %slice.18), channel_id=1, source_target_pairs={{0,16},{8,72},{16,0},{24,88},{32,48},{40,104},{48,32},{56,120},{64... | collective-permute-start | bytes 98312 | tf_op jit(solution)/shard_map/ppermute | solution.py:278
  47.6 5.6 %collective-permute-start.4 = (f32[16,128]{1,0:T(8,128)S(1)}, f32[16,128]{1,0:T(8,128)S(1)}, u32[]{:S(2)}, u32[]{:S(2)}) collective-permute-start(f32[16,128]{1,0:T(8,128)S(1)} %slice.19.mine_ref), channel_id=1, source_target_pairs={{0,8},{8,0},{16,24},{24,16},{32,40},{40,32},{48,56},{56,48},{64,72... | collective-permute-start | bytes 24584 | tf_op jit(solution)/shard_map/ppermute | solution.py:284
  55.7 1.4 %collective-permute-start.5 = (f32[128,128]{1,0:T(8,128)S(1)}, f32[128,128]{1,0:T(8,128)S(1)}, u32[]{:S(2)}, u32[]{:S(2)}) collective-permute-start(f32[128,128]{1,0:T(8,128)S(1)} %pad_maximum_fusion.1.mine_ref), channel_id=1, source_target_pairs={{0,8},{8,0},{16,24},{24,16},{32,40},{40,32},{48,56},{56,48},{64,72... | collective-permute-start | bytes 196616 | tf_op jit(solution)/shard_map/ppermute | solution.py:289

commit v9 on v8

--- a/solution.py
+++ b/solution.py
@@ -206,21 +206,33 @@
         out_ref[8 * g : 8 * g + 8, :] = block[:, :64]
 
 
-def apply_kernel(parts, inverse_ref, mine_ref, other_ref, out_ref):
+def solve(inverse_ref, columns):
+    return lax.dot_general(
+        inverse_ref[...],
+        columns,
+        (((1,), (0,)), ((), ())),
+        precision=lax.Precision.HIGHEST,
+        preferred_element_type=jnp.float32,
+    )
+
+
+def own_kernel(inverse_ref, mine_ref, out_ref):
+    rows = out_ref.shape[0]
+    out_ref[...] = solve(
+        inverse_ref, jnp.concatenate([mine_ref[:rows], mine_ref[rows:]], axis=1)
+    )
+
+
+def apply_kernel(parts, inverse_ref, own_ref, other_ref, out_ref):
     rows, share = out_ref.shape
     core, kept, across = place()
-    mine = [mine_ref[:rows], mine_ref[rows:]]
-    other = [other_ref[:rows], other_ref[rows:]]
+    other = solve(inverse_ref, jnp.concatenate([other_ref[:rows], other_ref[rows:]], axis=1))
+    mine = [own_ref[:, :128], own_ref[:, 128:]]
+    other = [other[:, :128], other[:, 128:]]
     mine = [jnp.where(kept == t, mine[0], mine[1]) for t in range(2)]
     other = [jnp.where(across == t, other[0], other[1]) for t in range(2)]
     tiles = [jnp.where(core == 0, p, q) for p, q in zip(mine + other, other + mine)]
-    solved = lax.dot_general(
-        inverse_ref[...],
-        jnp.concatenate(tiles, axis=1),
-        (((1,), (0,)), ((), ())),
-        precision=lax.Precision.HIGHEST,
-        preferred_element_type=jnp.float32,
-    )
+    solved = jnp.concatenate(tiles, axis=1)
     extra = lax.axis_index("narrow") * share % 16
     for shift in sorted({z * share % 16 for z in range(parts)}):
 
@@ -287,12 +299,13 @@
     beside, inverse = lax.optimization_barrier((beside, inverse))
     mine = jnp.concatenate([ours, beside], axis=0)
     other = near(lax.ppermute(mine, "wide", swap))
+    own = small(own_kernel, (rows, SPAN), "own", near(inverse), near(mine), space=pltpu.VMEM)
     return small(
         functools.partial(apply_kernel, parts),
         (rows, genes // parts),
         "apply",
         near(inverse),
-        near(mine),
+        near(own),
         other,
     )
 

time: 58.2 us -> 58.1 us (level)
    pallas_call x2 -> x3, Pallas kernels: 3.44 us -> 3.55 us  [small(): pl.pallas_call(kernel, in_specs=[pl.BlockSpec(memory_space=pltpu.VMEM)] *...]
  transfers between devices with their start and end apart: 6 -> 6, of which waited for: 3 -> 3; matrix products, arithmetic and copies ran while one was open for 0% -> 0% of each run, Pallas kernels for 10% -> 11%
where the time goes in v9:
time: 58.1 us; the launch traced here: 57.9 us
  blocking collectives  31.2 us (54%)
  Pallas kernels  12.8 us (22%)
  starting transfers between devices  9.18 us (16%)
  waiting for transfers between devices  4.32 us (7%)
    all_to_all x1, blocking collectives, on_device(): piece = lax.all_to_all(piece, 'narrow', 0, 0, tiled=True).sum(axis=0)  17.3 us
    all_to_all x1, blocking collectives, on_device(): lax.all_to_all(spread, 'wide', 0, 0, axis_index_groups=groups, tiled=True)  14 us
    pallas_call x1, Pallas kernels, begin(): pl.pallas_call(functools.partial(begin_kernel, parts, genes // parts), in...  5.72 us
    ppermute x1, starting transfers between devices, on_device(): lax.ppermute(square, 'wide', swap)  4.77 us
    pallas_call x3, Pallas kernels, small(): pl.pallas_call(kernel, in_specs=[pl.BlockSpec(memory_space=pltpu.VMEM)] *...  3.55 us
    pallas_call x3, Pallas kernels, more(): pl.pallas_call(functools.partial(more_kernel, which, parts, genes // part...  3.52 us
    ppermute x1, starting transfers between devices, on_device(): theirs = lax.ppermute(theirs, 'wide', swap)  3.33 us
    ppermute x1, waiting for transfers between devices, on_device(): given = lax.ppermute(give, 'wide', pairs)  2.78 us
  transfers between devices with their start and end apart: 6, of which 3 were waited for; matrix products, arithmetic and copies ran while one was open for 0% of the time, Pallas kernels for 11%

profile of v9, /device:TPU:1, one launch (start us, length us, event | category | flops | bytes accessed | tf_op | source)
XLA Modules:
  0.0 57.9 jit_solution(5663813710733777840)
XLA Ops:
  0.0 5.7 %begin.1 = (f32[528,128]{1,0:T(8,128)S(1)}, bf16[64,1536]{1,0:T(8,128)(2,1)S(1)}, f32[2,16,128]{2,1,0:T(8,128)S(1)}, bf16[4000,1536]{1,0:T(8,128)(2,1)S(1)}) custom-call(bf16[64,4000]{1,0:T(8,128)(2,1)} %s_hbm.1, bf16[4000,1536]{1,0:T(8,128)(2,1)} %e_hbm.1), custom_call_target="tpu_custom_call" | custom-call | tf_op jit(solution)/shard_map/begin/pallas_call | solution.py:98
  5.7 3.3 %collective-permute-start = (f32[528,128]{1,0:T(8,128)S(1)}, f32[528,128]{1,0:T(8,128)S(1)}, u32[]{:S(2)}, u32[]{:S(2)}) collective-permute-start(f32[528,128]{1,0:T(8,128)S(1)} %get-tuple-element.16), channel_id=1, source_target_pairs={{0,8},{8,0},{16,24},{24,16},{32,40},{40,32},{48,56},{56,48},{64,72... | collective-permute-start | bytes 811016 | tf_op jit(solution)/shard_map/ppermute | solution.py:275
  9.1 1.2 %give.1 = f32[528,128]{1,0:T(8,128)S(1)} custom-call(bf16[64,1536]{1,0:T(8,128)(2,1)S(1)} %get-tuple-element.13.sketched_ref, f32[2,16,128]{2,1,0:T(8,128)S(1)} %get-tuple-element.17.gram_ref, bf16[4000,1536]{1,0:T(8,128)(2,1)S(1)} %get-tuple-element.15.e_ref), custom_call_target="tpu_custom_call" | custom-call | flops 196608000 | bytes 6144000 | tf_op jit(solution)/shard_map/give/pallas_call | solution.py:124
  10.2 0.0 collective-permute-done
  10.3 0.1 collective-permute-start.1
  10.4 1.2 %theirs.1 = f32[528,128]{1,0:T(8,128)S(1)} custom-call(bf16[64,1536]{1,0:T(8,128)(2,1)S(1)} %get-tuple-element.13.sketched_ref, f32[2,16,128]{2,1,0:T(8,128)S(1)} %get-tuple-element.17.gram_ref, bf16[4000,1536]{1,0:T(8,128)(2,1)S(1)} %get-tuple-element.15.e_ref), custom_call_target="tpu_custom_call" | custom-call | flops 196608000 | bytes 6144000 | tf_op jit(solution)/shard_map/theirs/pallas_call | solution.py:124
  11.6 0.4 collective-permute-start.2
  12.0 1.2 %keep.1 = f32[528,128]{1,0:T(8,128)S(1)} custom-call(bf16[64,1536]{1,0:T(8,128)(2,1)S(1)} %get-tuple-element.13.sketched_ref, f32[2,16,128]{2,1,0:T(8,128)S(1)} %get-tuple-element.17.gram_ref, bf16[4000,1536]{1,0:T(8,128)(2,1)S(1)} %get-tuple-element.15.e_ref), custom_call_target="tpu_custom_call" | custom-call | flops 196608000 | bytes 6144000 | tf_op jit(solution)/shard_map/keep/pallas_call | solution.py:124
  13.2 2.8 %collective-permute-done.1 = f32[528,128]{1,0:T(8,128)S(1)} collective-permute-done((f32[528,128]{1,0:T(8,128)S(1)}, f32[528,128]{1,0:T(8,128)S(1)}, u32[]{:S(2)}, u32[]{:S(2)}) %collective-permute-start.1) | collective-permute-done | bytes 270368 | tf_op jit(solution)/shard_map/ppermute | solution.py:278
  16.0 0.0 collective-permute-done.2
  16.1 17.3 %all_to_all.10 = f32[8,80,128]{2,1,0:T(8,128)S(1)} all-to-all(f32[8,80,128]{2,1,0:T(8,128)S(1)} %pad_maximum_fusion), channel_id=1, replica_groups=mesh['wide'=32,'narrow'=8] {'narrow'}, dimensions={0} | all-to-all | bytes 655360 | tf_op jit(solution)/shard_map/all_to_all | solution.py:285
  33.5 14.0 %all_to_all.11 = f32[8,80,128]{2,1,0:T(8,128)S(1)} all-to-all(f32[8,80,128]{2,1,0:T(8,128)S(1)} %broadcast_in_dim.5), channel_id=1, replica_groups={{0,48,64,112,128,176,192,240},{16,32,80,96,144,160,208,224},{8,200,24,2..., dimensions={0} | all-to-all | bytes 655360 | tf_op jit(solution)/shard_map/all_to_all | solution.py:287
  47.5 0.1 collective-permute-start.3
  47.6 4.8 %collective-permute-start.4 = (f32[16,128]{1,0:T(8,128)S(1)}, f32[16,128]{1,0:T(8,128)S(1)}, u32[]{:S(2)}, u32[]{:S(2)}) collective-permute-start(f32[16,128]{1,0:T(8,128)S(1)} %slice.19.mine_ref), channel_id=1, source_target_pairs={{0,8},{8,0},{16,24},{24,16},{32,40},{40,32},{48,56},{56,48},{64,72... | collective-permute-start | bytes 24584 | tf_op jit(solution)/shard_map/ppermute | solution.py:296
  52.4 0.8 %collective-permute-done.4.other_ref = f32[16,128]{1,0:T(8,128)S(1)} collective-permute-done((f32[16,128]{1,0:T(8,128)S(1)}, f32[16,128]{1,0:T(8,128)S(1)}, u32[]{:S(2)}, u32[]{:S(2)}) %collective-permute-start.4) | collective-permute-done | bytes 8224 | tf_op jit(solution)/shard_map/ppermute | solution.py:296
  53.2 2.5 %factor.1.inverse_ref = f32[64,64]{1,0:T(8,128)S(1)} custom-call(f32[16,128]{1,0:T(8,128)S(1)} %slice.19.mine_ref, f32[16,128]{1,0:T(8,128)S(1)} %collective-permute-done.4.other_ref), custom_call_target="tpu_custom_call" | custom-call | tf_op jit(solution)/shard_map/factor/pallas_call | solution.py:138
  55.7 0.0 collective-permute-done.3
  55.7 0.5 collective-permute-start.5
  56.2 0.2 own.1.own_ref
  56.4 0.7 %collective-permute-done.5.other_ref = f32[128,128]{1,0:T(8,128)S(1)} collective-permute-done((f32[128,128]{1,0:T(8,128)S(1)}, f32[128,128]{1,0:T(8,128)S(1)}, u32[]{:S(2)}, u32[]{:S(2)}) %collective-permute-start.5) | collective-permute-done | bytes 65568 | tf_op jit(solution)/shard_map/ppermute | solution.py:301
  57.1 0.9 %apply.1 = f32[64,500]{1,0:T(8,128)} custom-call(f32[64,64]{1,0:T(8,128)S(1)} %factor.1.inverse_ref, f32[64,256]{1,0:T(8,128)S(1)} %own.1.own_ref, f32[128,128]{1,0:T(8,128)S(1)} %collective-permute-done.5.other_ref), custom_call_target="tpu_custom_call" | custom-call | tf_op jit(solution)/shard_map/apply/pallas_call | solution.py:138
  (13 shorter events, 0.2 us)
Async XLA Ops:
  5.7 4.5 %collective-permute-start = (f32[528,128]{1,0:T(8,128)S(1)}, f32[528,128]{1,0:T(8,128)S(1)}, u32[]{:S(2)}, u32[]{:S(2)}) collective-permute-start(f32[528,128]{1,0:T(8,128)S(1)} %get-tuple-element.16), channel_id=1, source_target_pairs={{0,8},{8,0},{16,24},{24,16},{32,40},{40,32},{48,56},{56,48},{64,72... | collective-permute-start | bytes 811016 | tf_op jit(solution)/shard_map/ppermute | solution.py:275
  10.3 5.7 %collective-permute-start.1 = (f32[528,128]{1,0:T(8,128)S(1)}, f32[528,128]{1,0:T(8,128)S(1)}, u32[]{:S(2)}, u32[]{:S(2)}) collective-permute-start(f32[528,128]{1,0:T(8,128)S(1)} %add.9), channel_id=1, source_target_pairs={{0,16},{8,72},{16,0},{24,88},{32,48},{40,104},{48,32},{56,120},{64... | collective-permute-start | bytes 811016 | tf_op jit(solution)/shard_map/ppermute | solution.py:278
  11.6 4.4 %collective-permute-start.2 = (f32[528,128]{1,0:T(8,128)S(1)}, f32[528,128]{1,0:T(8,128)S(1)}, u32[]{:S(2)}, u32[]{:S(2)}) collective-permute-start(f32[528,128]{1,0:T(8,128)S(1)} %theirs.1), channel_id=1, source_target_pairs={{0,8},{8,0},{16,24},{24,16},{32,40},{40,32},{48,56},{56,48},{64,72... | collective-permute-start | bytes 811016 | tf_op jit(solution)/shard_map/ppermute | solution.py:279
  47.5 8.2 %collective-permute-start.3 = (f32[64,128]{1,0:T(8,128)S(1)}, f32[64,128]{1,0:T(8,128)S(1)}, u32[]{:S(2)}, u32[]{:S(2)}) collective-permute-start(f32[64,128]{1,0:T(8,128)S(1)} %slice.18), channel_id=1, source_target_pairs={{0,16},{8,72},{16,0},{24,88},{32,48},{40,104},{48,32},{56,120},{64... | collective-permute-start | bytes 98312 | tf_op jit(solution)/shard_map/ppermute | solution.py:290
  47.6 5.6 %collective-permute-start.4 = (f32[16,128]{1,0:T(8,128)S(1)}, f32[16,128]{1,0:T(8,128)S(1)}, u32[]{:S(2)}, u32[]{:S(2)}) collective-permute-start(f32[16,128]{1,0:T(8,128)S(1)} %slice.19.mine_ref), channel_id=1, source_target_pairs={{0,8},{8,0},{16,24},{24,16},{32,40},{40,32},{48,56},{56,48},{64,72... | collective-permute-start | bytes 24584 | tf_op jit(solution)/shard_map/ppermute | solution.py:296
  55.7 1.4 %collective-permute-start.5 = (f32[128,128]{1,0:T(8,128)S(1)}, f32[128,128]{1,0:T(8,128)S(1)}, u32[]{:S(2)}, u32[]{:S(2)}) collective-permute-start(f32[128,128]{1,0:T(8,128)S(1)} %pad_maximum_fusion.1.mine_ref), channel_id=1, source_target_pairs={{0,8},{8,0},{16,24},{24,16},{32,40},{40,32},{48,56},{56,48},{64,72... | collective-permute-start | bytes 196616 | tf_op jit(solution)/shard_map/ppermute | solution.py:301

commit v10 on v8

--- a/solution.py
+++ b/solution.py
@@ -276,24 +276,20 @@
     total = spread.sum(axis=0)
     ours, square = total[:rows], total[rows:]
     beside = lax.ppermute(ours, "wide", pairs)
+    theirs = lax.ppermute(total, "wide", swap)
     inverse = small(
-        factor_kernel,
-        (rows, rows),
-        "factor",
-        near(square),
-        near(lax.ppermute(square, "wide", swap)),
-        space=pltpu.VMEM,
+        factor_kernel, (rows, rows), "factor", near(square), near(theirs[rows:]), space=pltpu.VMEM
     )
     beside, inverse = lax.optimization_barrier((beside, inverse))
     mine = jnp.concatenate([ours, beside], axis=0)
-    other = near(lax.ppermute(mine, "wide", swap))
+    other = jnp.concatenate([theirs[:rows], lax.ppermute(beside, "wide", swap)], axis=0)
     return small(
         functools.partial(apply_kernel, parts),
         (rows, genes // parts),
         "apply",
         near(inverse),
         near(mine),
-        other,
+        near(other),
     )
 
 

time: 58.2 us -> 58.2 us (level)
  no operation moved by 1% of the time
where the time goes in v10:
time: 58.2 us; the launch traced here: 58.1 us
  blocking collectives  31.2 us (54%)
  Pallas kernels  12.7 us (22%)
  starting transfers between devices  9.56 us (16%)
  waiting for transfers between devices  4.21 us (7%)
    all_to_all x1, blocking collectives, on_device(): piece = lax.all_to_all(piece, 'narrow', 0, 0, tiled=True).sum(axis=0)  17.3 us
    all_to_all x1, blocking collectives, on_device(): lax.all_to_all(spread, 'wide', 0, 0, axis_index_groups=groups, tiled=True)  14 us
    pallas_call x1, Pallas kernels, begin(): pl.pallas_call(functools.partial(begin_kernel, parts, genes // parts), in...  5.72 us
    ppermute x1, starting transfers between devices, on_device(): theirs = lax.ppermute(total, 'wide', swap)  4.77 us
    pallas_call x3, Pallas kernels, more(): pl.pallas_call(functools.partial(more_kernel, which, parts, genes // part...  3.52 us
    pallas_call x2, Pallas kernels, small(): pl.pallas_call(kernel, in_specs=[pl.BlockSpec(memory_space=pltpu.VMEM)] *...  3.45 us
    ppermute x1, starting transfers between devices, on_device(): theirs = lax.ppermute(theirs, 'wide', swap)  3.33 us
    ppermute x1, waiting for transfers between devices, on_device(): given = lax.ppermute(give, 'wide', pairs)  2.78 us
  transfers between devices with their start and end apart: 6, of which 3 were waited for; matrix products, arithmetic and copies ran while one was open for 0% of the time, Pallas kernels for 10%

profile of v10, /device:TPU:1, one launch (start us, length us, event | category | flops | bytes accessed | tf_op | source)
XLA Modules:
  0.0 58.1 jit_solution(1978243639995513763)
XLA Ops:
  0.0 5.7 %begin.1 = (f32[528,128]{1,0:T(8,128)S(1)}, bf16[64,1536]{1,0:T(8,128)(2,1)S(1)}, f32[2,16,128]{2,1,0:T(8,128)S(1)}, bf16[4000,1536]{1,0:T(8,128)(2,1)S(1)}) custom-call(bf16[64,4000]{1,0:T(8,128)(2,1)} %s_hbm.1, bf16[4000,1536]{1,0:T(8,128)(2,1)} %e_hbm.1), custom_call_target="tpu_custom_call" | custom-call | tf_op jit(solution)/shard_map/begin/pallas_call | solution.py:98
  5.7 3.3 %collective-permute-start = (f32[528,128]{1,0:T(8,128)S(1)}, f32[528,128]{1,0:T(8,128)S(1)}, u32[]{:S(2)}, u32[]{:S(2)}) collective-permute-start(f32[528,128]{1,0:T(8,128)S(1)} %get-tuple-element.16), channel_id=1, source_target_pairs={{0,8},{8,0},{16,24},{24,16},{32,40},{40,32},{48,56},{56,48},{64,72... | collective-permute-start | bytes 811016 | tf_op jit(solution)/shard_map/ppermute | solution.py:263
  9.1 1.2 %give.1 = f32[528,128]{1,0:T(8,128)S(1)} custom-call(bf16[64,1536]{1,0:T(8,128)(2,1)S(1)} %get-tuple-element.13.sketched_ref, f32[2,16,128]{2,1,0:T(8,128)S(1)} %get-tuple-element.17.gram_ref, bf16[4000,1536]{1,0:T(8,128)(2,1)S(1)} %get-tuple-element.15.e_ref), custom_call_target="tpu_custom_call" | custom-call | flops 196608000 | bytes 6144000 | tf_op jit(solution)/shard_map/give/pallas_call | solution.py:124
  10.2 0.0 collective-permute-done
  10.3 0.1 collective-permute-start.1
  10.4 1.2 %theirs.1 = f32[528,128]{1,0:T(8,128)S(1)} custom-call(bf16[64,1536]{1,0:T(8,128)(2,1)S(1)} %get-tuple-element.13.sketched_ref, f32[2,16,128]{2,1,0:T(8,128)S(1)} %get-tuple-element.17.gram_ref, bf16[4000,1536]{1,0:T(8,128)(2,1)S(1)} %get-tuple-element.15.e_ref), custom_call_target="tpu_custom_call" | custom-call | flops 196608000 | bytes 6144000 | tf_op jit(solution)/shard_map/theirs/pallas_call | solution.py:124
  11.6 0.4 collective-permute-start.2
  12.0 1.2 %keep.1 = f32[528,128]{1,0:T(8,128)S(1)} custom-call(bf16[64,1536]{1,0:T(8,128)(2,1)S(1)} %get-tuple-element.13.sketched_ref, f32[2,16,128]{2,1,0:T(8,128)S(1)} %get-tuple-element.17.gram_ref, bf16[4000,1536]{1,0:T(8,128)(2,1)S(1)} %get-tuple-element.15.e_ref), custom_call_target="tpu_custom_call" | custom-call | flops 196608000 | bytes 6144000 | tf_op jit(solution)/shard_map/keep/pallas_call | solution.py:124
  13.2 2.8 %collective-permute-done.1 = f32[528,128]{1,0:T(8,128)S(1)} collective-permute-done((f32[528,128]{1,0:T(8,128)S(1)}, f32[528,128]{1,0:T(8,128)S(1)}, u32[]{:S(2)}, u32[]{:S(2)}) %collective-permute-start.1) | collective-permute-done | bytes 270368 | tf_op jit(solution)/shard_map/ppermute | solution.py:266
  16.0 0.0 collective-permute-done.2
  16.1 17.3 %all_to_all.10 = f32[8,80,128]{2,1,0:T(8,128)S(1)} all-to-all(f32[8,80,128]{2,1,0:T(8,128)S(1)} %pad_maximum_fusion), channel_id=1, replica_groups=mesh['wide'=32,'narrow'=8] {'narrow'}, dimensions={0} | all-to-all | bytes 655360 | tf_op jit(solution)/shard_map/all_to_all | solution.py:273
  33.5 14.0 %all_to_all.11 = f32[8,80,128]{2,1,0:T(8,128)S(1)} all-to-all(f32[8,80,128]{2,1,0:T(8,128)S(1)} %broadcast_in_dim.5), channel_id=1, replica_groups={{0,48,64,112,128,176,192,240},{16,32,80,96,144,160,208,224},{8,200,24,2..., dimensions={0} | all-to-all | bytes 655360 | tf_op jit(solution)/shard_map/all_to_all | solution.py:275
  47.5 4.8 %collective-permute-start.4 = (f32[80,128]{1,0:T(8,128)S(1)}, f32[80,128]{1,0:T(8,128)S(1)}, u32[]{:S(2)}, u32[]{:S(2)}) collective-permute-start(f32[80,128]{1,0:T(8,128)S(1)} %reduce_sum.19), channel_id=1, source_target_pairs={{0,8},{8,0},{16,24},{24,16},{32,40},{40,32},{48,56},{56,48},{64,72... | collective-permute-start | bytes 122888 | tf_op jit(solution)/shard_map/ppermute | solution.py:279
  52.2 0.3 collective-permute-start.3
  52.5 0.6 collective-permute-done.4
  53.1 2.5 %factor.1.inverse_ref = f32[64,64]{1,0:T(8,128)S(1)} custom-call(f32[16,128]{1,0:T(8,128)S(1)} %slice.27.mine_ref, f32[16,128]{1,0:T(8,128)S(1)} %slice.28.other_ref), custom_call_target="tpu_custom_call" | custom-call | tf_op jit(solution)/shard_map/factor/pallas_call | solution.py:138
  55.6 0.0 collective-permute-done.3
  55.6 0.6 %collective-permute-start.5 = (f32[64,128]{1,0:T(8,128)S(1)}, f32[64,128]{1,0:T(8,128)S(1)}, u32[]{:S(2)}, u32[]{:S(2)}) collective-permute-start(f32[64,128]{1,0:T(8,128)S(1)} %collective-permute-done.3), channel_id=1, source_target_pairs={{0,8},{8,0},{16,24},{24,16},{32,40},{40,32},{48,56},{56,48},{64,72... | collective-permute-start | bytes 98312 | tf_op jit(solution)/shard_map/ppermute | solution.py:285
  56.3 0.8 %collective-permute-done.5 = f32[64,128]{1,0:T(8,128)S(1)} collective-permute-done((f32[64,128]{1,0:T(8,128)S(1)}, f32[64,128]{1,0:T(8,128)S(1)}, u32[]{:S(2)}, u32[]{:S(2)}) %collective-permute-start.5) | collective-permute-done | bytes 32800 | tf_op jit(solution)/shard_map/ppermute | solution.py:285
  57.1 0.9 %apply.1 = f32[64,500]{1,0:T(8,128)} custom-call(f32[64,64]{1,0:T(8,128)S(1)} %factor.1.inverse_ref, f32[128,128]{1,0:T(8,128)S(1)} %pad_maximum_fusion.1.mine_ref, f32[128,128]{1,0:T(8,128)S(1)} %pad_maximum_fusion.2.other_ref), custom_call_target="tpu_custom_call" | custom-call | tf_op jit(solution)/shard_map/apply/pallas_call | solution.py:138
  (16 shorter events, 0.2 us)
Async XLA Ops:
  5.7 4.5 %collective-permute-start = (f32[528,128]{1,0:T(8,128)S(1)}, f32[528,128]{1,0:T(8,128)S(1)}, u32[]{:S(2)}, u32[]{:S(2)}) collective-permute-start(f32[528,128]{1,0:T(8,128)S(1)} %get-tuple-element.16), channel_id=1, source_target_pairs={{0,8},{8,0},{16,24},{24,16},{32,40},{40,32},{48,56},{56,48},{64,72... | collective-permute-start | bytes 811016 | tf_op jit(solution)/shard_map/ppermute | solution.py:263
  10.3 5.7 %collective-permute-start.1 = (f32[528,128]{1,0:T(8,128)S(1)}, f32[528,128]{1,0:T(8,128)S(1)}, u32[]{:S(2)}, u32[]{:S(2)}) collective-permute-start(f32[528,128]{1,0:T(8,128)S(1)} %add.9), channel_id=1, source_target_pairs={{0,16},{8,72},{16,0},{24,88},{32,48},{40,104},{48,32},{56,120},{64... | collective-permute-start | bytes 811016 | tf_op jit(solution)/shard_map/ppermute | solution.py:266
  11.6 4.4 %collective-permute-start.2 = (f32[528,128]{1,0:T(8,128)S(1)}, f32[528,128]{1,0:T(8,128)S(1)}, u32[]{:S(2)}, u32[]{:S(2)}) collective-permute-start(f32[528,128]{1,0:T(8,128)S(1)} %theirs.1), channel_id=1, source_target_pairs={{0,8},{8,0},{16,24},{24,16},{32,40},{40,32},{48,56},{56,48},{64,72... | collective-permute-start | bytes 811016 | tf_op jit(solution)/shard_map/ppermute | solution.py:267
  47.5 5.6 %collective-permute-start.4 = (f32[80,128]{1,0:T(8,128)S(1)}, f32[80,128]{1,0:T(8,128)S(1)}, u32[]{:S(2)}, u32[]{:S(2)}) collective-permute-start(f32[80,128]{1,0:T(8,128)S(1)} %reduce_sum.19), channel_id=1, source_target_pairs={{0,8},{8,0},{16,24},{24,16},{32,40},{40,32},{48,56},{56,48},{64,72... | collective-permute-start | bytes 122888 | tf_op jit(solution)/shard_map/ppermute | solution.py:279
  52.2 3.4 %collective-permute-start.3 = (f32[64,128]{1,0:T(8,128)S(1)}, f32[64,128]{1,0:T(8,128)S(1)}, u32[]{:S(2)}, u32[]{:S(2)}) collective-permute-start(f32[64,128]{1,0:T(8,128)S(1)} %slice.26), channel_id=1, source_target_pairs={{0,16},{8,72},{16,0},{24,88},{32,48},{40,104},{48,32},{56,120},{64... | collective-permute-start | bytes 98312 | tf_op jit(solution)/shard_map/ppermute | solution.py:278
  55.6 1.5 %collective-permute-start.5 = (f32[64,128]{1,0:T(8,128)S(1)}, f32[64,128]{1,0:T(8,128)S(1)}, u32[]{:S(2)}, u32[]{:S(2)}) collective-permute-start(f32[64,128]{1,0:T(8,128)S(1)} %collective-permute-done.3), channel_id=1, source_target_pairs={{0,8},{8,0},{16,24},{24,16},{32,40},{40,32},{48,56},{56,48},{64,72... | collective-permute-start | bytes 98312 | tf_op jit(solution)/shard_map/ppermute | solution.py:285
